TPU v7x, 32 devices: a whole 2x2x4 slice. The times are simulated.
32 devices in a mesh: dp: 8 (over z, y), tp: 4 (over x, core).
Axes of the slice: x: 2, y: 2, z: 4, core: 2. Of those that a mesh axis runs over, the one named last changes fastest.
Arguments:
- frames: bfloat16 [16, 2304, 384], P('dp', 'tp'), may hold values from -6 to 6
- targets: bfloat16 [16, 2304, 384], P('dp', 'tp'), may hold values from -6 to 6
- presence: int32 [16, 4], P('dp'), may hold values 0 or 1
- order: int32 [8, 2], P('dp'), may hold values from 0 to 1, each once within a row
- attn_proj: float32 [3, 384, 384], P(None, None, 'tp'), may hold values from -0.3125 to 0.3125
- out_proj: float32 [384, 384], P('tp'), may hold values from -7 to 7
- up_proj: float32 [384, 1536], P(None, 'tp'), may hold values from -0.3125 to 0.3125
- up_bias: float32 [1536], P('tp'), may hold values from -3 to 3
- down_proj: float32 [384, 1536], P(None, 'tp'), may hold values from -0.15625 to 0.15625
- head_proj: float32 [384, 384], replicated, may hold values from -0.3125 to 0.3125
- vectors: float32 [9, 384], replicated
- momentum_attn: float32 [3, 384, 384], P(None, None, 'tp'), may hold values from -256 to 256
- momentum_out: float32 [384, 384], P('tp'), may hold values from -3 to 3
- momentum_up: float32 [384, 1536], P(None, 'tp'), may hold values from -3 to 3
- momentum_bias: float32 [1536], P('tp'), may hold values from -3 to 3
- momentum_down: float32 [384, 1536], P(None, 'tp'), may hold values from -3 to 3
- momentum_head: float32 [384, 384], replicated, may hold values from -224 to 224
- momentum_vectors: float32 [9, 384], replicated, may hold values from -3 to 3
- average_attn: float32 [3, 384, 384], P(None, None, 'tp'), may hold values from -0.3125 to 0.3125
- average_out: float32 [384, 384], P('tp'), may hold values from -7 to 7
- average_up: float32 [384, 1536], P(None, 'tp'), may hold values from -0.3125 to 0.3125
- average_bias: float32 [1536], P('tp'), may hold values from -3 to 3
- average_down: float32 [384, 1536], P(None, 'tp'), may hold values from -0.15625 to 0.15625
- average_head: float32 [384, 384], replicated, may hold values from -0.3125 to 0.3125
- average_vectors: float32 [9, 384], replicated
Outputs:
- loss: float32 [], replicated
- new_attn: float32 [3, 384, 384], P(None, None, 'tp')
- new_out: float32 [384, 384], P('tp')
- new_up: float32 [384, 1536], P(None, 'tp')
- new_bias: float32 [1536], P('tp')
- new_down: float32 [384, 1536], P(None, 'tp')
- new_head: float32 [384, 384], replicated
- new_vectors: float32 [9, 384], replicated
- moment_attn: float32 [3, 384, 384], P(None, None, 'tp')
- moment_out: float32 [384, 384], P('tp')
- moment_up: float32 [384, 1536], P(None, 'tp')
- moment_bias: float32 [1536], P('tp')
- moment_down: float32 [384, 1536], P(None, 'tp')
- moment_head: float32 [384, 384], replicated
- moment_vectors: float32 [9, 384], replicated
- mean_attn: float32 [3, 384, 384], P(None, None, 'tp')
- mean_out: float32 [384, 384], P('tp')
- mean_up: float32 [384, 1536], P(None, 'tp')
- mean_bias: float32 [1536], P('tp')
- mean_down: float32 [384, 1536], P(None, 'tp')
- mean_head: float32 [384, 384], replicated
- mean_vectors: float32 [9, 384], replicated
- grad_frames: float32 [16, 2304, 384], P('dp', 'tp')
Inputs may be any that keep to these rules, and one draw needn't show every extreme that they name: `order`: each row holds every number below 2 once.
All inputs are finite; a program needn't handle non-finite values. No bound on the sum of `presence` on one device may be relied on, other than what follows from the above.
Results may differ from a plain program's by a relative error of at most 0.0095.
Values may be sent and summed in bfloat16 or wider, within the bound.
No kernel may reach another device: no remote copies, remote signals or barrier semaphores. Data moves between devices by JAX's collectives and lax.ppermute only.
A program may use at most 192 MiB of HBM per device.

v0:
```python
import jax
import jax.numpy as jnp
from jax import lax
from jax.sharding import PartitionSpec as P

CHN = 96
HDIM = 48
HEAD = 384


EPSILON = 1e-05
MOMENTUM_RATE = 0.9
LEARN_RATE = 0.02
AVERAGE_RATE = 0.9


def product(left, right, form):
    return jnp.einsum(form, left, right, preferred_element_type=jnp.float32)


def norm_forward(values, gain, shift):
    centred = values - jnp.mean(values, axis=-1, keepdims=True)
    inverse = lax.rsqrt(jnp.mean(centred * centred, axis=-1, keepdims=True) + EPSILON)
    normed = centred * inverse
    return (normed * gain + shift, normed, inverse)


def norm_backward(grad, normed, inverse, gain):
    scaled = grad * gain
    back = inverse * (
        scaled
        - jnp.mean(scaled, axis=-1, keepdims=True)
        - normed * jnp.mean(scaled * normed, axis=-1, keepdims=True)
    )
    return (back, jnp.sum(grad * normed, axis=(0, 1)), jnp.sum(grad, axis=(0, 1)))


def head_forward(packed):
    query_rows, key_rows, value_rows = packed
    scores = product(query_rows, key_rows, "qd,kd->qk") * HDIM ** (-0.5)
    maximum = jnp.max(scores, axis=-1, keepdims=True)
    exponent = jnp.exp(scores - maximum)
    totals = jnp.sum(exponent, axis=-1, keepdims=True)
    weights = (exponent / totals).astype(jnp.bfloat16)
    mixed = product(weights, value_rows, "qk,kd->qd").astype(jnp.bfloat16)
    return (mixed, (maximum + jnp.log(totals))[:, 0])


def head_backward(packed):
    query_rows, key_rows, value_rows, logsum, grad_out = packed
    factor = HDIM ** (-0.5)
    probs = jnp.exp(product(query_rows, key_rows, "qd,kd->qk") * factor - logsum[:, None])
    grad_value = product(probs.astype(jnp.bfloat16), grad_out, "qk,qd->kd")
    grad_probs = product(grad_out, value_rows, "qd,kd->qk")
    grad_scores = (
        probs * (grad_probs - jnp.sum(probs * grad_probs, axis=-1, keepdims=True))
    ).astype(jnp.bfloat16)
    grad_query = product(grad_scores, key_rows, "qk,kd->qd") * factor
    grad_key = product(grad_scores, query_rows, "qk,qd->kd") * factor
    return jnp.stack([grad_query, grad_key, grad_value]).astype(jnp.bfloat16)


def to_heads(packed, items, heads_here):
    length = packed.shape[2]
    split = packed.reshape(3, items, length, heads_here, HDIM).transpose(0, 1, 3, 2, 4)
    return split.reshape(3, items * heads_here, length, HDIM)


def from_heads(stacked, items, heads_here):
    length = stacked.shape[-2]
    split = stacked.reshape(stacked.shape[:-3] + (items, heads_here, length, HDIM))
    moved = jnp.moveaxis(split, -2, -3)
    return moved.reshape(stacked.shape[:-3] + (items, length, heads_here * HDIM))


def update(weight, moment, average, grad):
    moment_new = MOMENTUM_RATE * moment + grad
    weight_new = weight - LEARN_RATE * (grad + MOMENTUM_RATE * moment_new)
    average_new = AVERAGE_RATE * average + (1.0 - AVERAGE_RATE) * weight_new
    return (weight_new, moment_new, average_new)


def per_device(
    frames,
    targets,
    presence,
    order,
    attn_proj,
    out_proj,
    up_proj,
    up_bias,
    down_proj,
    head_proj,
    vectors,
    momentum_attn,
    momentum_out,
    momentum_up,
    momentum_bias,
    momentum_down,
    momentum_head,
    momentum_vectors,
    average_attn,
    average_out,
    average_up,
    average_bias,
    average_down,
    average_head,
    average_vectors,
):
    items = frames.shape[0]
    heads_here = out_proj.shape[0] // HDIM
    bf16 = jnp.bfloat16
    start = frames.astype(jnp.float32)
    goal = jnp.take(targets, order[0], axis=0).astype(jnp.float32)
    keep = (presence.astype(jnp.float32)[:, :, None] * jnp.ones((1, 1, CHN), jnp.float32)).reshape(
        items, 1, HEAD
    )
    head_low = head_proj.astype(bf16)
    attn_low = attn_proj.astype(bf16)
    out_low = out_proj.astype(bf16)
    first, hat_one, inv_one = norm_forward(start, vectors[0], vectors[1])
    first_low = first.astype(bf16)
    first_all = lax.all_gather(first_low, "tp", axis=1, tiled=True)
    packed = product(first_all, attn_low, "bsd,jde->jbse").astype(bf16)
    heads = to_heads(packed, items, heads_here)
    mixed, logsum = lax.map(head_forward, (heads[0], heads[1], heads[2]))
    attended = from_heads(mixed, items, heads_here)
    attn_term = lax.psum_scatter(
        product(attended, out_low, "bse,ed->bsd"), "tp", scatter_dimension=1, tiled=True
    )
    middle = start + vectors[3] * (attn_term + vectors[2])
    second, hat_two, inv_two = norm_forward(middle, vectors[4], vectors[5])
    second_low = second.astype(bf16)
    up_all = up_proj.astype(bf16)
    down_all = down_proj.astype(bf16)
    second_all = lax.all_gather(second_low, "tp", axis=1, tiled=True)
    hidden_pre = product(second_all, up_all, "bsd,df->bsf") + up_bias
    hidden = jax.nn.gelu(hidden_pre).astype(bf16)
    ffn_term = lax.psum_scatter(
        product(hidden, down_all, "bsf,df->bsd"), "tp", scatter_dimension=1, tiled=True
    )
    final = middle + vectors[7] * (ffn_term + vectors[6])
    final_low = final.astype(bf16)
    pred = product(final_low, head_low, "bsd,dh->bsh") + vectors[8]
    diff = pred - goal
    smooth = jnp.sqrt(diff * diff + 1.0)
    part_loss = jnp.sum(keep * (smooth - 1.0)) / HEAD
    grad_pred = (keep * (diff / smooth) / HEAD).astype(bf16)
    grad_head = product(final_low, grad_pred, "bsd,bsh->dh")
    grad_head_bias = jnp.sum(grad_pred.astype(jnp.float32), axis=(0, 1))
    grad_final = product(grad_pred, head_low, "bsh,dh->bsd")
    grad_scale_two = jnp.sum(grad_final * (ffn_term + vectors[6]), axis=(0, 1))
    grad_ffn = grad_final * vectors[7]
    grad_down_bias = jnp.sum(grad_ffn, axis=(0, 1))
    ffn_low = grad_ffn.astype(bf16)
    gelu_pull = jax.vjp(jax.nn.gelu, hidden_pre)[1]
    ffn_all = lax.all_gather(ffn_low, "tp", axis=1, tiled=True)
    grad_hidden = product(ffn_all, down_all, "bsd,df->bsf")
    grad_down = product(ffn_all, hidden, "bsd,bsf->df")
    grad_pre = gelu_pull(grad_hidden)[0].astype(bf16)
    grad_up = product(second_all, grad_pre, "bsd,bsf->df")
    grad_up_bias = jnp.sum(grad_pre.astype(jnp.float32), axis=(0, 1))
    grad_second = lax.psum_scatter(
        product(grad_pre, up_all, "bsf,df->bsd"), "tp", scatter_dimension=1, tiled=True
    )
    back_two, grad_gain_two, grad_shift_two = norm_backward(
        grad_second, hat_two, inv_two, vectors[4]
    )
    grad_middle = grad_final + back_two
    grad_scale_one = jnp.sum(grad_middle * (attn_term + vectors[2]), axis=(0, 1))
    grad_attn = grad_middle * vectors[3]
    grad_out_bias = jnp.sum(grad_attn, axis=(0, 1))
    attn_grad_low = grad_attn.astype(bf16)
    attn_all = lax.all_gather(attn_grad_low, "tp", axis=1, tiled=True)
    grad_out = product(attended, attn_all, "bse,bsd->ed")
    grad_attended = product(attn_all, out_low, "bsd,ed->bse").astype(bf16)
    grad_mixed = to_heads(jnp.stack([grad_attended] * 3), items, heads_here)[0]
    grad_heads = lax.map(head_backward, (heads[0], heads[1], heads[2], logsum, grad_mixed))
    grad_packed = from_heads(jnp.moveaxis(grad_heads, 1, 0), items, heads_here)
    grad_attn_proj = product(first_all, grad_packed, "bsd,jbse->jde")
    grad_first = lax.psum_scatter(
        product(grad_packed, attn_low, "jbse,jde->bsd").astype(jnp.bfloat16),
        "tp",
        scatter_dimension=1,
        tiled=True,
    ).astype(jnp.float32)
    back_one, grad_gain_one, grad_shift_one = norm_backward(
        grad_first, hat_one, inv_one, vectors[0]
    )
    grad_frames = grad_middle + back_one
    grad_vectors = jnp.stack(
        [
            grad_gain_one,
            grad_shift_one,
            grad_out_bias,
            grad_scale_one,
            grad_gain_two,
            grad_shift_two,
            grad_down_bias,
            grad_scale_two,
            grad_head_bias,
        ]
    )
    grad_attn_proj, grad_out, grad_up, grad_up_bias, grad_down = lax.psum(
        (grad_attn_proj, grad_out, grad_up, grad_up_bias, grad_down), "dp"
    )
    grad_head, grad_vectors, loss = lax.psum((grad_head, grad_vectors, part_loss), ("dp", "tp"))
    first_set = update(attn_proj, momentum_attn, average_attn, grad_attn_proj)
    second_set = update(out_proj, momentum_out, average_out, grad_out)
    third_set = update(up_proj, momentum_up, average_up, grad_up)
    fourth_set = update(up_bias, momentum_bias, average_bias, grad_up_bias)
    fifth_set = update(down_proj, momentum_down, average_down, grad_down)
    sixth_set = update(head_proj, momentum_head, average_head, grad_head)
    seventh_set = update(vectors, momentum_vectors, average_vectors, grad_vectors)
    return (
        loss,
        first_set[0],
        second_set[0],
        third_set[0],
        fourth_set[0],
        fifth_set[0],
        sixth_set[0],
        seventh_set[0],
        first_set[1],
        second_set[1],
        third_set[1],
        fourth_set[1],
        fifth_set[1],
        sixth_set[1],
        seventh_set[1],
        first_set[2],
        second_set[2],
        third_set[2],
        fourth_set[2],
        fifth_set[2],
        sixth_set[2],
        seventh_set[2],
        grad_frames,
    )


def solution(mesh):
    in_specs = (
        P("dp", "tp", None),
        P("dp", "tp", None),
        P("dp", None),
        P("dp", None),
        P(None, None, "tp"),
        P("tp", None),
        P(None, "tp"),
        P("tp"),
        P(None, "tp"),
        P(),
        P(),
        P(None, None, "tp"),
        P("tp", None),
        P(None, "tp"),
        P("tp"),
        P(None, "tp"),
        P(),
        P(),
        P(None, None, "tp"),
        P("tp", None),
        P(None, "tp"),
        P("tp"),
        P(None, "tp"),
        P(),
        P(),
    )
    out_specs = (
        P(),
        P(None, None, "tp"),
        P("tp", None),
        P(None, "tp"),
        P("tp"),
        P(None, "tp"),
        P(),
        P(),
        P(None, None, "tp"),
        P("tp", None),
        P(None, "tp"),
        P("tp"),
        P(None, "tp"),
        P(),
        P(),
        P(None, None, "tp"),
        P("tp", None),
        P(None, "tp"),
        P("tp"),
        P(None, "tp"),
        P(),
        P(),
        P("dp", "tp", None),
    )
    return jax.shard_map(
        per_device, mesh=mesh, in_specs=in_specs, out_specs=out_specs, check_vma=False
    )
```

profile of v0, /device:TPU:0, one launch (start us, length us, event | category | flops | bytes accessed | tf_op | source)
XLA Modules:
  0.0 926.1 jit_solution(6012306189877405584)
XLA Ops:
  14.3 33.5 %all-gather.5.cloned.1.call-done = bf16[2,2304,384]{2,1,0:T(8,128)(2,1)} async-done(((bf16[2,576,384]{2,1,0:T(8,128)(2,1)}), bf16[2,2304,384]{2,1,0:T(8,128)(2,1)}) %all-gather.5.cloned.1.call-update) | async-done | bytes 3538960 | tf_op jit(solution)/shard_map/all_gather | solution.py:123
  61.8 57.2 %while.22 = (s32[]{:T(128)}, bf16[4,2304,48]{1,2,0:T(8,128)(2,1)}, f32[4,2304]{1,0:T(4,128)}, bf16[4,2304,48]{2,1,0:T(8,128)(2,1)S(1)}, bf16[4,2304,48]{2,1,0:T(...) while((s32[]{:T(128)}, bf16[4,2304,48]{1,2,0:T(8,128)(2,1)}, f32[4,2304]{1,0:T(4,128)}, ...), condition=%wide.region_5.6_spmd, body=%wide.region_2.0_spmd.sunk | while | flops 1056483072 | bytes 65804384 | solution.py:126
  61.8 4.0 fusion.141
  68.9 5.8 fusion.143
  76.1 4.0 fusion.141
  83.1 5.8 fusion.143
  90.4 4.0 fusion.141
  97.4 5.8 fusion.143
  104.7 4.0 fusion.141
  111.7 5.8 fusion.143
  119.0 5.8 fusion.97
  124.9 63.7 %reduce-scatter.5.cloned.1.call-done = f32[2,576,384]{2,1,0:T(8,128)} async-done(((f32[2,2304,384]{2,1,0:T(8,128)}), f32[2,576,384]{2,1,0:T(8,128)}) %reduce-scatter.5.cloned.1.call-update) | async-done | bytes 1769488 | tf_op jit(solution)/shard_map/reduce_scatter | solution.py:128
  192.9 30.4 %all-gather.7.cloned.1.call-done = bf16[2,2304,384]{2,1,0:T(8,128)(2,1)} async-done(((bf16[2,576,384]{2,1,0:T(8,128)(2,1)}), bf16[2,2304,384]{2,1,0:T(8,128)(2,1)}) %all-gather.7.cloned.1.call-update) | async-done | bytes 3538960 | tf_op jit(solution)/shard_map/all_gather | solution.py:136
  223.3 4.4 fusion.84
  230.6 4.8 fusion.80
  237.9 61.4 %reduce-scatter.7.cloned.1.call-done = f32[2,576,384]{2,1,0:T(8,128)} async-done(((f32[2,2304,384]{2,1,0:T(8,128)}), f32[2,576,384]{2,1,0:T(8,128)}) %reduce-scatter.7.cloned.1.call-update) | async-done | bytes 1769488 | tf_op jit(solution)/shard_map/reduce_scatter | solution.py:139
  307.0 30.7 %all-gather.9.cloned.1.call-done = bf16[2,2304,384]{2,1,0:T(8,128)(2,1)} async-done(((bf16[2,576,384]{2,1,0:T(8,128)(2,1)}), bf16[2,2304,384]{2,1,0:T(8,128)(2,1)}) %all-gather.9.cloned.1.call-update) | async-done | bytes 3538960 | tf_op jit(solution)/shard_map/all_gather | solution.py:157
  337.7 10.0 %convert_reduce_fusion = (f32[384]{0:T(512)}, bf16[2,2304,384]{2,1,0:T(8,128)(2,1)S(1)}) fusion(f32[2,2304,384]{2,1,0:T(8,128)} %copy-done.17, f32[384]{0:T(512)S(1)} %copy-done.71, bf16[2,2304,384]{2,1,0:T(8,128)(2,1)} %all-gather.9.cloned.1.call-done, f32[384,384]{1,0:T(8,128)} %param.37), kind=kOutput, calls=%fused_computation.64 | convolution fusion | flops 1399799424 | bytes 14748672 | tf_op jit(solution)/shard_map/bsd,df->bsf/dot_general | solution.py:18
  349.5 4.3 fusion.82
  353.9 63.8 %reduce-scatter.9.cloned.1.call-done = f32[2,576,384]{2,1,0:T(8,128)} async-done(((f32[2,2304,384]{2,1,0:T(8,128)}), f32[2,576,384]{2,1,0:T(8,128)}) %reduce-scatter.9.cloned.1.call-update) | async-done | bytes 1769488 | tf_op jit(solution)/shard_map/reduce_scatter | solution.py:163
  427.8 8.2 convolution_bitcast_fusion.1
  438.8 18.2 %all-gather.11.cloned.1.call-done = bf16[2,2304,384]{2,1,0:T(8,128)(2,1)} async-done(((bf16[2,576,384]{2,1,0:T(8,128)(2,1)}), bf16[2,2304,384]{2,1,0:T(8,128)(2,1)}) %all-gather.11.cloned.1.call-update) | async-done | bytes 3538960 | tf_op jit(solution)/shard_map/all_gather | solution.py:174
  463.2 263.6 %while.23 = (s32[]{:T(128)}, bf16[4,3,2304,48]{2,3,1,0:T(8,128)(2,1)}, bf16[4,2304,48]{2,1,0:T(8,128)(2,1)S(1)}, bf16[4,2304,48]{2,1,0:T(8,128)(2,1)}, f32[4,230...) while((s32[]{:T(128)}, ...), condition=%wide.region_17.18_spmd, body=%wide.region_15.17_spmd.sunk | while | flops 2593048320 | bytes 211429520 | solution.py:178
  464.0 11.5 %fusion.152 = f32[2304,2304]{0,1:T(8,128)} fusion(bf16[4,2304,48]{2,1,0:T(8,128)(2,1)} %get-tuple-element.366, s32[]{:T(128)S(6)} %copy.111, bf16[4,2304,48]{2,1,0:T(8,128)(2,1)} %get-tuple-element.365), kind=kOutput, calls=%fused_computation.33.clone.1 | convolution fusion | flops 509607936 | bytes 22414336 | tf_op jit(solution)/shard_map/while/body/eval_jaxpr/qd,kd->qk/dot_general | solution.py:18
  475.5 13.6 %multiply_reduce_fusion.11 = (f32[2304]{0:T(1024)S(1)}, f32[2304,2304]{0,1:T(8,128)}) fusion(f32[2304,2304]{0,1:T(8,128)} %fusion.152, f32[2304]{0:T(1024)S(1)} %dynamic-slice_reduce_fusion.2, bf16[4,2304,48]{2,1,0:T(8,128)(2,1)S(1)} %copy-done.5, s32[]{:T(128)S(6)} %copy.111, bf16[4,2304,48]{2,1,0:T(8,128)(2,1)S(1)} %get-tuple-element.362), kind=kOutput, calls=%fused_computation.20.clone.1 | convolution fusion | flops 530839296 | bytes 43669504 | tf_op jit(solution)/shard_map/while/body/eval_jaxpr/qd,kd->qk/dot_general | solution.py:18
  489.1 18.4 %multiply_convert_fusion.9 = bf16[2304,2304]{0,1:T(8,128)(2,1)} fusion(f32[2304,2304]{0,1:T(8,128)} %get-tuple-element.318, f32[2304,2304]{0,1:T(8,128)} %fusion.152, f32[2304]{0:T(1024)S(1)} %get-tuple-element.319), kind=kLoop, calls=%fused_computation.19.clone.1 | loop fusion | flops 15925248 | bytes 53093376 | tf_op jit(solution)/shard_map/while/body/eval_jaxpr/convert_element_type | solution.py:57
  507.5 10.5 %fusion.153 = bf16[1,1,2304,48]{2,3,1,0:T(8,128)(2,1)S(1)} fusion(f32[2304,2304]{0,1:T(8,128)} %get-tuple-element.318, bf16[4,2304,48]{2,1,0:T(8,128)(2,1)} %get-tuple-element.365, s32[]{:T(128)S(6)} %copy.111), kind=kOutput, calls=%fused_computation.31.clone.1 | convolution fusion | flops 515026944 | bytes 22044676 | tf_op jit(solution)/shard_map/while/body/eval_jaxpr/qk,qd->kd/dot_general | solution.py:18
  518.0 6.2 fusion.155
  530.2 11.4 %fusion.152 = f32[2304,2304]{0,1:T(8,128)} fusion(bf16[4,2304,48]{2,1,0:T(8,128)(2,1)} %get-tuple-element.366, s32[]{:T(128)S(6)} %copy.111, bf16[4,2304,48]{2,1,0:T(8,128)(2,1)} %get-tuple-element.365), kind=kOutput, calls=%fused_computation.33.clone.1 | convolution fusion | flops 509607936 | bytes 22414336 | tf_op jit(solution)/shard_map/while/body/eval_jaxpr/qd,kd->qk/dot_general | solution.py:18
  541.6 13.6 %multiply_reduce_fusion.11 = (f32[2304]{0:T(1024)S(1)}, f32[2304,2304]{0,1:T(8,128)}) fusion(f32[2304,2304]{0,1:T(8,128)} %fusion.152, f32[2304]{0:T(1024)S(1)} %dynamic-slice_reduce_fusion.2, bf16[4,2304,48]{2,1,0:T(8,128)(2,1)S(1)} %copy-done.5, s32[]{:T(128)S(6)} %copy.111, bf16[4,2304,48]{2,1,0:T(8,128)(2,1)S(1)} %get-tuple-element.362), kind=kOutput, calls=%fused_computation.20.clone.1 | convolution fusion | flops 530839296 | bytes 43669504 | tf_op jit(solution)/shard_map/while/body/eval_jaxpr/qd,kd->qk/dot_general | solution.py:18
  555.2 18.4 %multiply_convert_fusion.9 = bf16[2304,2304]{0,1:T(8,128)(2,1)} fusion(f32[2304,2304]{0,1:T(8,128)} %get-tuple-element.318, f32[2304,2304]{0,1:T(8,128)} %fusion.152, f32[2304]{0:T(1024)S(1)} %get-tuple-element.319), kind=kLoop, calls=%fused_computation.19.clone.1 | loop fusion | flops 15925248 | bytes 53093376 | tf_op jit(solution)/shard_map/while/body/eval_jaxpr/convert_element_type | solution.py:57
  573.5 10.5 %fusion.153 = bf16[1,1,2304,48]{2,3,1,0:T(8,128)(2,1)S(1)} fusion(f32[2304,2304]{0,1:T(8,128)} %get-tuple-element.318, bf16[4,2304,48]{2,1,0:T(8,128)(2,1)} %get-tuple-element.365, s32[]{:T(128)S(6)} %copy.111), kind=kOutput, calls=%fused_computation.31.clone.1 | convolution fusion | flops 515026944 | bytes 22044676 | tf_op jit(solution)/shard_map/while/body/eval_jaxpr/qk,qd->kd/dot_general | solution.py:18
  584.0 6.2 fusion.155
  596.1 11.4 %fusion.152 = f32[2304,2304]{0,1:T(8,128)} fusion(bf16[4,2304,48]{2,1,0:T(8,128)(2,1)} %get-tuple-element.366, s32[]{:T(128)S(6)} %copy.111, bf16[4,2304,48]{2,1,0:T(8,128)(2,1)} %get-tuple-element.365), kind=kOutput, calls=%fused_computation.33.clone.1 | convolution fusion | flops 509607936 | bytes 22414336 | tf_op jit(solution)/shard_map/while/body/eval_jaxpr/qd,kd->qk/dot_general | solution.py:18
  607.5 13.5 %multiply_reduce_fusion.11 = (f32[2304]{0:T(1024)S(1)}, f32[2304,2304]{0,1:T(8,128)}) fusion(f32[2304,2304]{0,1:T(8,128)} %fusion.152, f32[2304]{0:T(1024)S(1)} %dynamic-slice_reduce_fusion.2, bf16[4,2304,48]{2,1,0:T(8,128)(2,1)S(1)} %copy-done.5, s32[]{:T(128)S(6)} %copy.111, bf16[4,2304,48]{2,1,0:T(8,128)(2,1)S(1)} %get-tuple-element.362), kind=kOutput, calls=%fused_computation.20.clone.1 | convolution fusion | flops 530839296 | bytes 43669504 | tf_op jit(solution)/shard_map/while/body/eval_jaxpr/qd,kd->qk/dot_general | solution.py:18
  621.0 18.3 %multiply_convert_fusion.9 = bf16[2304,2304]{0,1:T(8,128)(2,1)} fusion(f32[2304,2304]{0,1:T(8,128)} %get-tuple-element.318, f32[2304,2304]{0,1:T(8,128)} %fusion.152, f32[2304]{0:T(1024)S(1)} %get-tuple-element.319), kind=kLoop, calls=%fused_computation.19.clone.1 | loop fusion | flops 15925248 | bytes 53093376 | tf_op jit(solution)/shard_map/while/body/eval_jaxpr/convert_element_type | solution.py:57
  639.3 10.4 %fusion.153 = bf16[1,1,2304,48]{2,3,1,0:T(8,128)(2,1)S(1)} fusion(f32[2304,2304]{0,1:T(8,128)} %get-tuple-element.318, bf16[4,2304,48]{2,1,0:T(8,128)(2,1)} %get-tuple-element.365, s32[]{:T(128)S(6)} %copy.111), kind=kOutput, calls=%fused_computation.31.clone.1 | convolution fusion | flops 515026944 | bytes 22044676 | tf_op jit(solution)/shard_map/while/body/eval_jaxpr/qk,qd->kd/dot_general | solution.py:18
  649.7 6.2 fusion.155
  661.8 11.4 %fusion.152 = f32[2304,2304]{0,1:T(8,128)} fusion(bf16[4,2304,48]{2,1,0:T(8,128)(2,1)} %get-tuple-element.366, s32[]{:T(128)S(6)} %copy.111, bf16[4,2304,48]{2,1,0:T(8,128)(2,1)} %get-tuple-element.365), kind=kOutput, calls=%fused_computation.33.clone.1 | convolution fusion | flops 509607936 | bytes 22414336 | tf_op jit(solution)/shard_map/while/body/eval_jaxpr/qd,kd->qk/dot_general | solution.py:18
  673.2 13.5 %multiply_reduce_fusion.11 = (f32[2304]{0:T(1024)S(1)}, f32[2304,2304]{0,1:T(8,128)}) fusion(f32[2304,2304]{0,1:T(8,128)} %fusion.152, f32[2304]{0:T(1024)S(1)} %dynamic-slice_reduce_fusion.2, bf16[4,2304,48]{2,1,0:T(8,128)(2,1)S(1)} %copy-done.5, s32[]{:T(128)S(6)} %copy.111, bf16[4,2304,48]{2,1,0:T(8,128)(2,1)S(1)} %get-tuple-element.362), kind=kOutput, calls=%fused_computation.20.clone.1 | convolution fusion | flops 530839296 | bytes 43669504 | tf_op jit(solution)/shard_map/while/body/eval_jaxpr/qd,kd->qk/dot_general | solution.py:18
  686.7 18.3 %multiply_convert_fusion.9 = bf16[2304,2304]{0,1:T(8,128)(2,1)} fusion(f32[2304,2304]{0,1:T(8,128)} %get-tuple-element.318, f32[2304,2304]{0,1:T(8,128)} %fusion.152, f32[2304]{0:T(1024)S(1)} %get-tuple-element.319), kind=kLoop, calls=%fused_computation.19.clone.1 | loop fusion | flops 15925248 | bytes 53093376 | tf_op jit(solution)/shard_map/while/body/eval_jaxpr/convert_element_type | solution.py:57
  705.0 10.4 %fusion.153 = bf16[1,1,2304,48]{2,3,1,0:T(8,128)(2,1)S(1)} fusion(f32[2304,2304]{0,1:T(8,128)} %get-tuple-element.318, bf16[4,2304,48]{2,1,0:T(8,128)(2,1)} %get-tuple-element.365, s32[]{:T(128)S(6)} %copy.111), kind=kOutput, calls=%fused_computation.31.clone.1 | convolution fusion | flops 515026944 | bytes 22044676 | tf_op jit(solution)/shard_map/while/body/eval_jaxpr/qk,qd->kd/dot_general | solution.py:18
  715.4 6.2 fusion.155
  733.4 4.9 bitcast_convert_fusion
  743.9 22.0 %psum.60 = f32[384]{0:T(512)S(1)} all-reduce(f32[384]{0:T(512)} %get-tuple-element.228), channel_id=1, replica_groups=mesh['dp'=8,'tp'=4] {'dp'}, use_global_device_ids=true, to_apply=%region_22.23 | all-reduce | flops 384 | bytes 3072 | tf_op jit(solution)/shard_map/psum | solution.py:204
  770.3 58.2 %all-reduce.7.cloned.1.call-done = (f32[3,384,96]{1,2,0:T(8,128)}, f32[96,384]{1,0:T(8,128)}, f32[384,384]{1,0:T(8,128)}, f32[384,384]{1,0:T(8,128)}) async-done(((f32[3,384,96]{1,2,0:T(8,128)}, f32[96,384]{1,0:T(8,128)}, f32[384,384]{1,0:T(8,128)}, f32[384,384]{1,0:T(8,128)}), (f32[3,384,96]{1,2,0:T(8,128)}, f32[96,384]{1,0:T(8,128)}, f32[384,384]{1,0:T(8,128)}, ...) | async-done | bytes 1769488 | tf_op jit(solution)/shard_map/psum | solution.py:204
  836.1 35.0 %reduce-scatter.11.cloned.1.call-done = bf16[2,576,384]{2,1,0:T(8,128)(2,1)} async-done(((bf16[2,2304,384]{2,1,0:T(8,128)(2,1)}), bf16[2,576,384]{2,1,0:T(8,128)(2,1)}) %reduce-scatter.11.cloned.1.call-update) | async-done | bytes 884752 | tf_op jit(solution)/shard_map/reduce_scatter | solution.py:181
  874.6 39.9 %all-reduce = (f32[]{:T(128)}, f32[9,384]{1,0:T(8,128)}) all-reduce(f32[]{:T(128)S(6)} %div.48, f32[9,384]{1,0:T(8,128)S(1)} %stack.61), channel_id=1, replica_groups=mesh['dp'=8,'tp'=4] {'dp','tp'}, use_global_device_ids=true, to_apply=%region_11.12 | all-reduce | flops 3457 | bytes 27656 | tf_op jit(solution)/shard_map/psum | solution.py:207
  (281 shorter events, 131.2 us)
Async XLA Ops:
  7.2 229.1 %copy-start = (bf16[2,576,384]{2,1,0:T(8,128)(2,1)S(1)}, bf16[2,576,384]{2,1,0:T(8,128)(2,1)}, u32[]{:S(2)}) copy-start(bf16[2,576,384]{2,1,0:T(8,128)(2,1)} %param.30) | copy-start | bytes 2654212
  7.2 40.6 %copy-start.41 = (f32[3,384,96]{1,2,0:T(8,128)S(1)}, f32[3,384,96]{1,2,0:T(8,128)}, u32[]{:S(2)}) copy-start(f32[3,384,96]{1,2,0:T(8,128)} %param.33) | copy-start | bytes 1327108
  7.2 40.6 %all-gather.5.cloned.1.call-start = ((), (), s32[]{:S(2)}) async-start(), calls=%async_computation.4 | async-start | bytes 4423680 | tf_op jit(solution)/shard_map/all_gather | solution.py:123
  14.2 174.4 %reduce-scatter.5.cloned.1.call-start = ((), (), s32[]{:S(2)}) async-start(), calls=%async_computation.5 | async-start | bytes 8847360 | tf_op jit(solution)/shard_map/reduce_scatter | solution.py:128
  61.8 57.2 %copy-start.23 = (f32[96,384]{1,0:T(8,128)S(1)}, f32[96,384]{1,0:T(8,128)}, u32[]{:S(2)}) copy-start(f32[96,384]{1,0:T(8,128)} %param.34) | copy-start | bytes 442372
  124.8 63.8 %copy-start.7 = (bf16[2,576,384]{2,1,0:T(8,128)(2,1)S(1)}, bf16[2,576,384]{2,1,0:T(8,128)(2,1)}, u32[]{:S(2)}) copy-start(bf16[2,576,384]{2,1,0:T(8,128)(2,1)} %param.29) | copy-start | bytes 2654212
  124.8 63.8 %copy-start.53 = (f32[384]{0:T(512)S(1)}, f32[384]{0:T(512)}, u32[]{:S(2)}) copy-start(f32[384]{0:T(512)} %get-tuple-element.155) | copy-start | bytes 4612
  124.8 63.8 %copy-start.57 = (f32[384]{0:T(512)S(1)}, f32[384]{0:T(512)}, u32[]{:S(2)}) copy-start(f32[384]{0:T(512)} %get-tuple-element.152) | copy-start | bytes 4612
  124.9 98.4 %all-gather.7.cloned.1.call-start = ((), (), s32[]{:S(2)}) async-start(), calls=%async_computation.6 | async-start | bytes 4423680 | tf_op jit(solution)/shard_map/all_gather | solution.py:136
  190.5 32.7 %copy-start.19 = (f32[384,384]{1,0:T(8,128)S(1)}, f32[384,384]{1,0:T(8,128)}, u32[]{:S(2)}) copy-start(f32[384,384]{1,0:T(8,128)} %param.35) | copy-start | bytes 1769476
  192.4 38.2 %copy-start.71 = (f32[384]{0:T(512)S(1)}, f32[384]{0:T(512)}, u32[]{:S(2)}) copy-start(f32[384]{0:T(512)} %param.36) | copy-start | bytes 4612
  192.4 107.0 %reduce-scatter.7.cloned.1.call-start = ((), (), s32[]{:S(2)}) async-start(), calls=%async_computation.7 | async-start | bytes 8847360 | tf_op jit(solution)/shard_map/reduce_scatter | solution.py:139
  235.4 63.9 %copy-start.55 = (f32[384]{0:T(512)S(1)}, f32[384]{0:T(512)}, u32[]{:S(2)}) copy-start(f32[384]{0:T(512)} %get-tuple-element.148) | copy-start | bytes 4612
  235.4 63.9 %copy-start.56 = (f32[384]{0:T(512)S(1)}, f32[384]{0:T(512)}, u32[]{:S(2)}) copy-start(f32[384]{0:T(512)} %get-tuple-element.151) | copy-start | bytes 4612
  235.4 102.3 %all-gather.9.cloned.1.call-start = ((), (), s32[]{:S(2)}) async-start(), calls=%async_computation.8 | async-start | bytes 4423680 | tf_op jit(solution)/shard_map/all_gather | solution.py:157
  237.9 63.3 %copy-start.21 = (f32[384,384]{1,0:T(8,128)S(1)}, f32[384,384]{1,0:T(8,128)}, u32[]{:S(2)}) copy-start(f32[384,384]{1,0:T(8,128)} %param.38) | copy-start | bytes 1769476
  237.9 63.3 %copy-start.72 = (f32[384]{0:T(512)S(1)}, f32[384]{0:T(512)}, u32[]{:S(2)}) copy-start(f32[384]{0:T(512)} %get-tuple-element.147) | copy-start | bytes 4612
  306.8 110.9 %reduce-scatter.9.cloned.1.call-start = ((), (), s32[]{:S(2)}) async-start(), calls=%async_computation.9 | async-start | bytes 8847360 | tf_op jit(solution)/shard_map/reduce_scatter | solution.py:163
  353.8 103.2 %all-gather.11.cloned.1.call-start = ((), (), s32[]{:S(2)}) async-start(), calls=%async_computation.10 | async-start | bytes 4423680 | tf_op jit(solution)/shard_map/all_gather | solution.py:174
  426.1 315.2 %all-reduce.5.cloned.1.call-start = ((), (), s32[]{:S(2)}) async-start(), calls=%async_computation.11 | async-start | bytes 1179648 | tf_op jit(solution)/shard_map/psum | solution.py:207
  427.7 400.7 %all-reduce.7.cloned.1.call-start = ((), (), s32[]{:S(2)}) async-start(), calls=%async_computation.13 | async-start | bytes 3538944 | tf_op jit(solution)/shard_map/psum | solution.py:204
  436.0 21.1 %copy-start.24 = (f32[96,384]{1,0:T(8,128)S(1)}, f32[96,384]{1,0:T(8,128)}, u32[]{:S(2)}) copy-start(f32[96,384]{1,0:T(8,128)} %param.34) | copy-start | bytes 442372
  464.0 11.5 %copy-start.5 = (bf16[4,2304,48]{2,1,0:T(8,128)(2,1)S(1)}, bf16[4,2304,48]{2,1,0:T(8,128)(2,1)}, u32[]{:S(2)}) copy-start(bf16[4,2304,48]{2,1,0:T(8,128)(2,1)} %get-tuple-element.363) | copy-start | bytes 2654212 | tf_op jit(solution)/shard_map/while
  733.4 137.7 %reduce-scatter.11.cloned.1.call-start = ((), (), s32[]{:S(2)}) async-start(), calls=%async_computation.12 | async-start | bytes 4423680 | tf_op jit(solution)/shard_map/reduce_scatter | solution.py:181
  738.4 29.0 %copy-start.62 = (f32[384]{0:T(512)S(1)}, f32[384]{0:T(512)}, u32[]{:S(2)}) copy-start(f32[384]{0:T(512)} %get-tuple-element.135) | copy-start | bytes 4612
  738.4 29.5 %copy-start.61 = (f32[384]{0:T(512)S(1)}, f32[384]{0:T(512)}, u32[]{:S(2)}) copy-start(f32[384]{0:T(512)} %get-tuple-element.142) | copy-start | bytes 4612
  738.4 31.3 %copy-start.63 = (f32[384]{0:T(512)S(1)}, f32[384]{0:T(512)}, u32[]{:S(2)}) copy-start(f32[384]{0:T(512)} %get-tuple-element.144) | copy-start | bytes 4612
  738.4 90.1 %copy-start.25 = (f32[96,384]{1,0:T(8,128)S(1)}, f32[96,384]{1,0:T(8,128)}, u32[]{:S(2)}) copy-start(f32[96,384]{1,0:T(8,128)} %param.34) | copy-start | bytes 442372
  738.4 90.1 %copy-start.45 = (f32[96,384]{1,0:T(8,128)S(1)}, f32[96,384]{1,0:T(8,128)}, u32[]{:S(2)}) copy-start(f32[96,384]{1,0:T(8,128)} %param.48) | copy-start | bytes 442372
  738.4 90.0 %copy-start.46 = (f32[96,384]{1,0:T(8,128)S(1)}, f32[96,384]{1,0:T(8,128)}, u32[]{:S(2)}) copy-start(f32[96,384]{1,0:T(8,128)} %param.41) | copy-start | bytes 442372
  741.3 88.9 %copy-start.42 = (f32[3,384,96]{1,2,0:T(8,128)S(1)}, f32[3,384,96]{1,2,0:T(8,128)}, u32[]{:S(2)}) copy-start(f32[3,384,96]{1,2,0:T(8,128)} %param.33) | copy-start | bytes 1327108
  741.3 88.9 %copy-start.43 = (f32[3,384,96]{1,2,0:T(8,128)S(1)}, f32[3,384,96]{1,2,0:T(8,128)}, u32[]{:S(2)}) copy-start(f32[3,384,96]{1,2,0:T(8,128)} %param.47) | copy-start | bytes 1327108
  741.4 88.9 %copy-start.44 = (f32[3,384,96]{1,2,0:T(8,128)S(1)}, f32[3,384,96]{1,2,0:T(8,128)}, u32[]{:S(2)}) copy-start(f32[3,384,96]{1,2,0:T(8,128)} %param.40) | copy-start | bytes 1327108
  743.9 88.5 %copy-start.20 = (f32[384,384]{1,0:T(8,128)S(1)}, f32[384,384]{1,0:T(8,128)}, u32[]{:S(2)}) copy-start(f32[384,384]{1,0:T(8,128)} %param.35) | copy-start | bytes 1769476
  743.9 88.5 %copy-start.33 = (f32[384,384]{1,0:T(8,128)S(1)}, f32[384,384]{1,0:T(8,128)}, u32[]{:S(2)}) copy-start(f32[384,384]{1,0:T(8,128)} %param.49) | copy-start | bytes 1769476
  743.9 88.5 %copy-start.34 = (f32[384,384]{1,0:T(8,128)S(1)}, f32[384,384]{1,0:T(8,128)}, u32[]{:S(2)}) copy-start(f32[384,384]{1,0:T(8,128)} %param.42) | copy-start | bytes 1769476
  833.9 37.2 %copy-start.8 = (bf16[2,576,384]{2,1,0:T(8,128)(2,1)S(1)}, bf16[2,576,384]{2,1,0:T(8,128)(2,1)}, u32[]{:S(2)}) copy-start(bf16[2,576,384]{2,1,0:T(8,128)(2,1)} %param.29) | copy-start | bytes 2654212
  833.9 37.2 %copy-start.48 = (f32[2,576]{1,0:T(2,128)S(1)}, f32[2,576]{1,0:T(2,128)}, u32[]{:S(2)}) copy-start(f32[2,576]{1,0:T(2,128)} %copy-done.47) | copy-start | bytes 13828
  833.9 37.2 %copy-start.50 = (f32[2,576]{1,0:T(2,128)S(1)}, f32[2,576]{1,0:T(2,128)}, u32[]{:S(2)}) copy-start(f32[2,576]{1,0:T(2,128)} %copy-done.49) | copy-start | bytes 13828
  833.9 37.2 %copy-start.52 = (f32[384]{0:T(512)S(1)}, f32[384]{0:T(512)}, u32[]{:S(2)}) copy-start(f32[384]{0:T(512)} %copy-done.51) | copy-start | bytes 4612
  834.7 39.3 %copy-start.64 = (f32[1,384]{1,0:T(1,128)S(1)}, f32[1,384]{1,0:T(1,128)}, u32[]{:S(2)}) copy-start(f32[1,384]{1,0:T(1,128)} %stack.60) | copy-start | bytes 4612
  834.7 39.3 %copy-start.65 = (f32[1,384]{1,0:T(1,128)S(1)}, f32[1,384]{1,0:T(1,128)}, u32[]{:S(2)}) copy-start(f32[1,384]{1,0:T(1,128)} %stack.59) | copy-start | bytes 4612
  834.7 39.3 %copy-start.66 = (f32[1,384]{1,0:T(1,128)S(1)}, f32[1,384]{1,0:T(1,128)}, u32[]{:S(2)}) copy-start(f32[1,384]{1,0:T(1,128)} %stack.58) | copy-start | bytes 4612
  834.7 39.3 %copy-start.67 = (f32[1,384]{1,0:T(1,128)S(1)}, f32[1,384]{1,0:T(1,128)}, u32[]{:S(2)}) copy-start(f32[1,384]{1,0:T(1,128)} %stack.56) | copy-start | bytes 4612
  834.7 39.3 %copy-start.68 = (f32[1,384]{1,0:T(1,128)S(1)}, f32[1,384]{1,0:T(1,128)}, u32[]{:S(2)}) copy-start(f32[1,384]{1,0:T(1,128)} %stack.57) | copy-start | bytes 4612
  834.7 39.3 %copy-start.69 = (f32[1,384]{1,0:T(1,128)S(1)}, f32[1,384]{1,0:T(1,128)}, u32[]{:S(2)}) copy-start(f32[1,384]{1,0:T(1,128)} %stack.55) | copy-start | bytes 4612
  834.7 39.3 %copy-start.70 = (f32[1,384]{1,0:T(1,128)S(1)}, f32[1,384]{1,0:T(1,128)}, u32[]{:S(2)}) copy-start(f32[1,384]{1,0:T(1,128)} %stack.54) | copy-start | bytes 4612
  834.7 81.3 %copy-start.13 = (f32[2,576,384]{2,1,0:T(8,128)S(1)}, f32[2,576,384]{2,1,0:T(8,128)}, u32[]{:S(2)}) copy-start(f32[2,576,384]{2,1,0:T(8,128)} %copy-done.12) | copy-start | bytes 5308420
  (45 other events, 172.2 us)
Sparse Core Ops, SparseCore 0:
  14.4 33.4 all-gather.4
  125.0 63.6 reduce-scatter.4
  192.5 30.7 all-gather.6
  235.6 63.7 reduce-scatter.6
  306.9 30.7 all-gather.8
  353.9 63.6 reduce-scatter.8
  426.3 30.7 all-gather.10
  463.7 127.3 all-reduce.4
  733.5 94.9 all-reduce.6
  831.0 40.0 reduce-scatter.10
where the time goes:
time: 936 us; the launch traced here: 926 us
  waiting for transfers between devices  395 us (42%)
  matrix products  282 us (30%)
  other arithmetic  126 us (13%)
  blocking collectives  62 us (7%)
  local copies, waits for them, and re-layouts  43.8 us (5%)
  between operations  16 us (2%)
    dot_general x43, matrix products, product(): return jnp.einsum(form, left, right, preferred_element_type=jnp.float32)  282 us
    convert_element_type x4, other arithmetic, head_backward(): grad_scores = (probs * (grad_probs - jnp.sum(probs * grad_probs, axis=-1,...  73.3 us
    reduce_scatter x1, waiting for transfers between devices, per_device(): lax.psum_scatter(product(grad_pre, up_all, 'bsf,df->bsd'), 'tp', scatter_...  63.8 us
    reduce_scatter x1, waiting for transfers between devices, per_device(): lax.psum_scatter(product(attended, out_low, 'bse,ed->bsd'), 'tp', scatter...  63.7 us
    reduce_scatter x1, waiting for transfers between devices, per_device(): lax.psum_scatter(product(hidden, down_all, 'bsf,df->bsd'), 'tp', scatter_...  61.4 us
    psum x1, waiting for transfers between devices, per_device(): lax.psum((grad_attn_proj, grad_out, grad_up, grad_up_bias, grad_down), 'dp')  58.2 us
    psum x1, blocking collectives, per_device(): lax.psum((grad_head, grad_vectors, part_loss), ('dp', 'tp'))  39.9 us
    reduce_scatter x1, waiting for transfers between devices, per_device(): lax.psum_scatter(product(grad_packed, attn_low, 'jbse,jde->bsd').astype(j...  35 us
  transfers between devices with their start and end apart: 10, of which 9 were waited for; matrix products, arithmetic and copies ran while one was open for 33% of the time, Pallas kernels for 0%

commit v1 on v0

v1 whole, which is shorter than its diff:
```python
import math

import jax
import jax.numpy as jnp
from jax import lax
from jax.experimental import pallas as pl
from jax.experimental.pallas import tpu as pltpu
from jax.sharding import PartitionSpec as P

CHN = 96
HDIM = 48
HPAD = 64
HEAD = 384


EPSILON = 1e-05
MOMENTUM_RATE = 0.9
LEARN_RATE = 0.02
AVERAGE_RATE = 0.9
SCALE = HDIM ** (-0.5)
LOG_SCALE = SCALE * math.log2(math.e)
VMEM_LIMIT = 56 << 20

bf16 = jnp.bfloat16
f32 = jnp.float32


def contract(left, right, left_dim, right_dim):
    return lax.dot_general(
        left, right, (((left_dim,), (right_dim,)), ((), ())), preferred_element_type=f32
    )


def attention_forward_body(query, key, value, mixed, totals, weights):
    scores = contract(query[...], key[...], 0, 0)
    maximum = jnp.max(scores, axis=1, keepdims=True)
    exponent = jnp.exp2((scores - maximum) * LOG_SCALE).astype(bf16)
    weights[0] = exponent
    summed = contract(value[...], exponent, 1, 1)
    total = summed[HDIM : HDIM + 1]
    mixed[...] = (summed[:HDIM] / total).astype(bf16)
    totals[0] = total


def attention_forward(query, key, value):
    heads = query.shape[0] // HDIM
    rows, length = query.shape[1], key.shape[1]
    return pl.pallas_call(
        attention_forward_body,
        grid=(heads,),
        in_specs=[
            pl.BlockSpec((HDIM, rows), lambda h: (h, 0)),
            pl.BlockSpec((HDIM, length), lambda h: (h, 0)),
            pl.BlockSpec((HPAD, length), lambda h: (h, 0)),
        ],
        out_specs=[
            pl.BlockSpec((HDIM, rows), lambda h: (h, 0)),
            pl.BlockSpec((1, 1, rows), lambda h: (h, 0, 0)),
            pl.BlockSpec((1, rows, length), lambda h: (h, 0, 0)),
        ],
        out_shape=[
            jax.ShapeDtypeStruct((heads * HDIM, rows), bf16),
            jax.ShapeDtypeStruct((heads, 1, rows), f32),
            jax.ShapeDtypeStruct((heads, rows, length), bf16),
        ],
        compiler_params=pltpu.CompilerParams(vmem_limit_bytes=VMEM_LIMIT),
        cost_estimate=pl.CostEstimate(
            flops=heads * rows * length * 4 * 256,
            bytes_accessed=heads * rows * length * 2,
            transcendentals=heads * rows * length,
        ),
        name="attention_forward",
    )(query, key, value)


def attention_backward_body(
    query, key, value, mixed, grad_mixed, totals, weights, grad_query, grad_key, grad_value
):
    inverse = 1.0 / totals[0]
    grad = grad_mixed[...].astype(f32)
    delta = jnp.sum(grad * mixed[...].astype(f32), axis=0, keepdims=True)
    scaled = (grad * inverse).astype(bf16)
    offset = -delta * inverse
    high = offset.astype(bf16).astype(f32)
    low = offset - high
    row = lax.broadcasted_iota(jnp.int32, (HPAD - HDIM, offset.shape[1]), 0)
    extra = jnp.where(row == 0, high, jnp.where(row == 1, low, 0.0)).astype(bf16)
    grad_weights = contract(jnp.concatenate([scaled, extra], axis=0), value[...], 0, 0)
    kept = weights[0]
    grad_scores = (kept.astype(f32) * grad_weights).astype(bf16)
    grad_query[...] = (contract(key[...], grad_scores, 1, 1) * SCALE).astype(bf16)
    grad_key[...] = (contract(query[...], grad_scores, 1, 0) * SCALE).astype(bf16)
    grad_value[...] = contract(scaled, kept, 1, 0).astype(bf16)


def attention_backward(first, heads, query, key, value, mixed, grad_mixed, totals, weights):
    rows, length = query.shape[1], key.shape[1]
    rows_in = pl.BlockSpec((HDIM, rows), lambda h: (h + first, 0))
    rows_spec = pl.BlockSpec((HDIM, rows), lambda h: (h, 0))
    length_spec = pl.BlockSpec((HDIM, length), lambda h: (h, 0))
    return pl.pallas_call(
        attention_backward_body,
        grid=(heads,),
        in_specs=[
            rows_in,
            pl.BlockSpec((HDIM, length), lambda h: (h + first, 0)),
            pl.BlockSpec((HPAD, length), lambda h: (h + first, 0)),
            rows_in,
            rows_spec,
            pl.BlockSpec((1, 1, rows), lambda h: (h + first, 0, 0)),
            pl.BlockSpec((1, rows, length), lambda h: (h + first, 0, 0)),
        ],
        out_specs=[rows_spec, length_spec, length_spec],
        out_shape=[
            jax.ShapeDtypeStruct((heads * HDIM, rows), bf16),
            jax.ShapeDtypeStruct((heads * HDIM, length), bf16),
            jax.ShapeDtypeStruct((heads * HDIM, length), bf16),
        ],
        compiler_params=pltpu.CompilerParams(vmem_limit_bytes=VMEM_LIMIT),
        cost_estimate=pl.CostEstimate(
            flops=heads * rows * length * 8 * 256,
            bytes_accessed=heads * rows * length * 2,
            transcendentals=0,
        ),
        name="attention_backward",
    )(query, key, value, mixed, grad_mixed, totals, weights)


GELU_A = math.sqrt(2.0 / math.pi)
GELU_B = 0.044715
SMALL = 16
BLOCK = 384


def split_small(values):
    high = values.astype(bf16)
    return high, (values - high.astype(f32)).astype(bf16)


def row_mean(values):
    return jnp.mean(values, axis=-1, keepdims=True)


def column_sum(values):
    return jnp.sum(values, axis=0, keepdims=True)


def middle_body(
    place,
    attended,
    frames,
    goal,
    keep,
    vectors,
    bias,
    out_low,
    up_low,
    down_low,
    head_low,
    grad_middle_out,
    grad_attended_out,
    kept_out,
    sent_out,
    sum_out,
    sum_up,
    sum_down,
    sum_head,
    sum_small,
    sum_bias,
):
    step = pl.program_id(0)

    @pl.when(step == 0)
    def _():
        for total in (sum_out, sum_up, sum_down, sum_head, sum_small, sum_bias):
            total[...] = jnp.zeros_like(total)

    gain, shift = vectors[4:5], vectors[5:6]
    scale_one, scale_two = vectors[3:4], vectors[7:8]
    biased_one = contract(attended[...], out_low[...], 0, 0) + vectors[2:3]
    middle = frames[...].astype(f32) + scale_one * biased_one
    centred = middle - row_mean(middle)
    inverse = lax.rsqrt(row_mean(centred * centred) + EPSILON)
    normed = centred * inverse
    second = (normed * gain + shift).astype(bf16)
    pre = contract(second, up_low[...], 1, 0) + bias[...]
    square = pre * pre
    tanh = jnp.tanh(GELU_A * (pre + GELU_B * square * pre))
    phi = 0.5 * (1.0 + tanh)
    hidden = (pre * phi).astype(bf16)
    slope = phi + pre * (0.5 * GELU_A) * (1.0 - tanh * tanh) * (1.0 + 3.0 * GELU_B * square)
    biased_two = contract(hidden, down_low[...], 1, 1) + vectors[6:7]
    final = middle + scale_two * biased_two
    final_low = final.astype(bf16)
    pred = contract(final_low, head_low[...], 1, 0) + vectors[8:9]
    diff = pred - goal[...].astype(f32)
    smooth = jnp.sqrt(diff * diff + 1.0)
    loss = column_sum(keep[...] * (smooth - 1.0)) / HEAD
    grad_pred = (keep[...] * (diff / smooth) / HEAD).astype(bf16)
    sum_head[...] += contract(final_low, grad_pred, 0, 0)
    grad_final = contract(grad_pred, head_low[...], 1, 1)
    grad_ffn = grad_final * scale_two
    ffn_low = grad_ffn.astype(bf16)
    grad_hidden = contract(ffn_low, down_low[...], 1, 0)
    sum_down[...] += contract(ffn_low, hidden, 0, 0)
    grad_pre = grad_hidden * slope
    pre_low = grad_pre.astype(bf16)
    sum_up[...] += contract(second, pre_low, 0, 0)
    sum_bias[...] += column_sum(pre_low.astype(f32))
    grad_second = contract(pre_low, up_low[...], 1, 1)
    scaled = grad_second * gain
    back = inverse * (scaled - row_mean(scaled) - normed * row_mean(scaled * normed))
    grad_middle = grad_final + back
    grad_attn = grad_middle * scale_one
    attn_low = grad_attn.astype(bf16)
    sum_out[...] += contract(attended[...], attn_low, 1, 0)
    grad_attended_out[...] = contract(out_low[...], attn_low, 1, 1).astype(bf16)
    grad_middle_out[...] = grad_middle
    rows = [
        column_sum(grad_attn),
        column_sum(grad_middle * biased_one),
        column_sum(grad_second * normed),
        column_sum(grad_second),
        column_sum(grad_ffn),
        column_sum(grad_final * biased_two),
        column_sum(grad_pred.astype(f32)),
        loss,
    ]
    sum_small[0:8] += jnp.concatenate(rows, axis=0)

    @pl.when(step == pl.num_programs(0) - 1)
    def _():
        share = sum_out.shape[0] // 4
        deep, width = sum_up.shape[0], sum_up.shape[1] // 4
        count = share + 2 * deep
        half = sum_head.shape[0] // 2
        core = lax.rem(place[0], 2)
        for j in range(4):
            target = (kept_out, sent_out)[j % 2]
            base = (j // 2) * count
            columns = slice(j * width, (j + 1) * width)
            target[base : base + share] = sum_out[j * share : (j + 1) * share].astype(bf16)
            target[base + share : base + share + deep] = sum_up[:, columns].astype(bf16)
            target[base + share + deep : base + count] = sum_down[:, columns].astype(bf16)
            sum_small[pl.ds(8 + lax.bitwise_xor(place[0], j), 1)] = sum_bias[:, columns]
        base = 2 * count
        kept_out[base : base + half] = sum_head[pl.ds(pl.multiple_of(core * half, half), half)].astype(bf16)
        sent_out[base : base + half] = sum_head[
            pl.ds(pl.multiple_of((1 - core) * half, half), half)
        ].astype(bf16)
        column = lax.broadcasted_iota(jnp.int32, (1, HEAD), 1)
        total = jnp.sum(sum_small[7:8], axis=1, keepdims=True)
        sum_small[7:8] = jnp.where(column == 0, total, 0.0)
        high, low = split_small(sum_small[...])
        for target in (kept_out, sent_out):
            target[base + half : base + half + SMALL] = high
            target[base + half + SMALL : base + half + 2 * SMALL] = low


def middle_step(
    place, attended, frames, goal, keep, vectors, bias, out_low, up_low, down_low, head_low
):
    rows, model = frames.shape
    share, wide = out_low.shape[0] // 4, up_low.shape[1]
    count = 2 * (share + 2 * model) + HEAD // 2 + 2 * SMALL

    def whole(array):
        return pl.BlockSpec(array.shape, lambda i, place: (0, 0))

    by_row = pl.BlockSpec((BLOCK, model), lambda i, place: (i, 0))
    by_column = pl.BlockSpec((model, BLOCK), lambda i, place: (0, i))
    payload = pl.BlockSpec((count, HEAD), lambda i, place: (0, 0))
    fixed = (keep, vectors, bias, out_low, up_low, down_low, head_low)
    return pl.pallas_call(
        middle_body,
        grid_spec=pltpu.PrefetchScalarGridSpec(
            num_scalar_prefetch=1,
            grid=(rows // BLOCK,),
            in_specs=[by_column, by_row, by_row] + [whole(a) for a in fixed],
            out_specs=[by_row, by_column, payload, payload],
            scratch_shapes=[
                pltpu.VMEM(out_low.shape, f32),
                pltpu.VMEM(up_low.shape, f32),
                pltpu.VMEM(down_low.shape, f32),
                pltpu.VMEM(head_low.shape, f32),
                pltpu.VMEM((SMALL, HEAD), f32),
                pltpu.VMEM((1, wide), f32),
            ],
        ),
        out_shape=[
            jax.ShapeDtypeStruct((rows, model), f32),
            jax.ShapeDtypeStruct((model, rows), bf16),
            jax.ShapeDtypeStruct((count, HEAD), bf16),
            jax.ShapeDtypeStruct((count, HEAD), bf16),
        ],
        compiler_params=pltpu.CompilerParams(vmem_limit_bytes=VMEM_LIMIT),
        cost_estimate=pl.CostEstimate(
            flops=rows * model * (12 * wide + 12 * model),
            bytes_accessed=10 * model * wide,
            transcendentals=rows * wide,
        ),
        name="middle_step",
    )(place, attended, frames, goal, *fixed)


def add_small(left, right, start):
    ends = [(r[start : start + SMALL].astype(f32), r[start + SMALL :].astype(f32)) for r in (left, right)]
    return (ends[0][0] + ends[0][1]) + (ends[1][0] + ends[1][1])


def add_rows(left, right, start, stop):
    return left[start:stop].astype(f32) + right[start:stop].astype(f32)


def fold_core_body(block, left, right, kept, sent):
    small = left.shape[0] - 2 * SMALL
    kept[:block] = add_rows(left, right, 0, block).astype(bf16)
    sent[:block] = add_rows(left, right, block, 2 * block).astype(bf16)
    shared = small - 2 * block
    high, low = split_small(add_small(left, right, small))
    for target in (kept, sent):
        if shared:
            target[block : block + shared] = add_rows(left, right, 2 * block, small).astype(bf16)
        target[block + shared : block + shared + SMALL] = high
        target[block + shared + SMALL :] = low


def fold_core(block, left, right):
    shape = jax.ShapeDtypeStruct((left.shape[0] - block, left.shape[1]), bf16)
    return pl.pallas_call(
        lambda *refs: fold_core_body(block, *refs),
        out_shape=[shape, shape],
        compiler_params=pltpu.CompilerParams(vmem_limit_bytes=VMEM_LIMIT),
        cost_estimate=pl.CostEstimate(flops=left.size, bytes_accessed=8 * left.size, transcendentals=0),
        name="fold_core",
    )(left, right)


def fold_body(left, right, total):
    small = left.shape[0] - 2 * SMALL
    both = add_small(left, right, small)
    total[:small] = add_rows(left, right, 0, small).astype(total.dtype)
    if total.dtype == f32:
        total[small:] = both
    else:
        high, low = split_small(both)
        total[small : small + SMALL] = high
        total[small + SMALL :] = low


def fold(left, right, last=False):
    rows = left.shape[0]
    shape = jax.ShapeDtypeStruct((rows - SMALL, left.shape[1]), f32) if last else left
    return pl.pallas_call(
        fold_body,
        out_shape=jax.ShapeDtypeStruct(shape.shape, shape.dtype),
        compiler_params=pltpu.CompilerParams(vmem_limit_bytes=VMEM_LIMIT),
        cost_estimate=pl.CostEstimate(flops=left.size, bytes_accessed=6 * left.size, transcendentals=0),
        name="fold",
    )(left, right)


def product(left, right, form):
    return jnp.einsum(form, left, right, preferred_element_type=jnp.float32)


def norm_forward(values, gain, shift):
    centred = values - jnp.mean(values, axis=-1, keepdims=True)
    inverse = lax.rsqrt(jnp.mean(centred * centred, axis=-1, keepdims=True) + EPSILON)
    normed = centred * inverse
    return (normed * gain + shift, normed, inverse)


def norm_backward(grad, normed, inverse, gain):
    scaled = grad * gain
    back = inverse * (
        scaled
        - jnp.mean(scaled, axis=-1, keepdims=True)
        - normed * jnp.mean(scaled * normed, axis=-1, keepdims=True)
    )
    return (back, jnp.sum(grad * normed, axis=0), jnp.sum(grad, axis=0))


def update(weight, moment, average, grad):
    moment_new = MOMENTUM_RATE * moment + grad
    weight_new = weight - LEARN_RATE * (grad + MOMENTUM_RATE * moment_new)
    average_new = AVERAGE_RATE * average + (1.0 - AVERAGE_RATE) * weight_new
    return (weight_new, moment_new, average_new)


CORE_PAIRS = [(0, 1), (1, 0), (2, 3), (3, 2)]
CHIP_PAIRS = [(0, 2), (2, 0), (1, 3), (3, 1)]


def swap_core(values):
    return lax.ppermute(values, "tp", CORE_PAIRS)


def swap_chip(values):
    return lax.ppermute(values, "tp", CHIP_PAIRS)


def swap_dp(values, step, size):
    return lax.ppermute(values, "dp", [(i, i ^ step) for i in range(size)])


def pick(stacked, place):
    return lax.dynamic_index_in_dim(stacked, place, 0, False)


def rounded(values):
    return lax.reduce_precision(values, 8, 7)


def two_part(values):
    high = rounded(values)
    return jnp.concatenate([high, rounded(values - high)], axis=0)


def per_device(
    frames,
    targets,
    presence,
    order,
    attn_proj,
    out_proj,
    up_proj,
    up_bias,
    down_proj,
    head_proj,
    vectors,
    momentum_attn,
    momentum_out,
    momentum_up,
    momentum_bias,
    momentum_down,
    momentum_head,
    momentum_vectors,
    average_attn,
    average_out,
    average_up,
    average_bias,
    average_down,
    average_head,
    average_vectors,
):
    size = lax.axis_size("dp")
    place = lax.axis_index("tp")
    chip, core = place // 2, place % 2
    width = up_proj.shape[1]
    own = pick(frames, chip)
    got = swap_chip(pick(frames, 1 - chip))
    mine = jnp.concatenate([own, got], axis=0)
    rows = mine.shape[0]
    theirs = swap_core(mine)
    every = jnp.concatenate([mine, theirs], axis=0)
    attn_own = jnp.swapaxes(attn_proj, 1, 2).astype(bf16)
    attn_core = swap_core(attn_own)
    attn_chip = swap_chip(attn_own)
    attn_both = swap_core(attn_chip)
    near = jnp.concatenate([attn_own, attn_core], axis=1)
    far = jnp.concatenate([attn_chip, attn_both], axis=1)
    rest = jnp.concatenate([out_proj, up_proj, down_proj], axis=0).astype(bf16)
    sent = jnp.concatenate([rest, pick(targets, order[0, 1 - chip])], axis=0)
    got_sent = swap_chip(sent)
    rest_rows = rest.shape[0]
    rest_core = swap_core(rest)
    rest_chip = got_sent[:rest_rows]
    rest_both = swap_core(rest_chip)
    blocks = [rest, rest_core, rest_chip, rest_both]
    share = out_proj.shape[0]
    deep = up_proj.shape[0]
    out_all = jnp.concatenate([b[:share] for b in blocks], axis=0)
    up_all = jnp.concatenate([b[share : share + deep] for b in blocks], axis=1)
    down_all = jnp.concatenate([b[share + deep :] for b in blocks], axis=1)
    bias_core = swap_core(up_bias)
    bias_chip = swap_chip(up_bias)
    bias_all = jnp.concatenate([up_bias, bias_core, bias_chip, swap_core(bias_chip)])
    goal = jnp.concatenate([pick(targets, order[0, chip]), got_sent[rest_rows:]], axis=0)
    keep = jnp.repeat(pick(presence, chip).astype(f32), CHN)[None, :]
    head_low = head_proj.astype(bf16)

    first, hat_all, inv_all = norm_forward(every.astype(f32), vectors[0], vectors[1])
    first_low = first.astype(bf16)
    start = mine.astype(f32)
    hat_one, inv_one = hat_all[:rows], inv_all[:rows]

    def project(block):
        query = product(block[0], first_low[:rows], "ed,nd->en").astype(bf16)
        key = product(block[1], first_low, "ed,nd->en").astype(bf16)
        value = product(block[2], first_low, "ed,nd->en").astype(bf16)
        heads = value.shape[0] // HDIM
        length = value.shape[1]
        ones = jnp.ones((heads, 2, length), bf16)
        zeros = jnp.zeros((heads, HPAD - HDIM - 2, length), bf16)
        value = jnp.concatenate([value.reshape(heads, HDIM, length), ones, zeros], axis=1)
        return query, key, value.reshape(heads * HPAD, length)

    inputs = [project(block) for block in (near, far)]
    outputs = [attention_forward(*part) for part in inputs]
    attended = jnp.concatenate([part[0] for part in outputs], axis=0)
    grad_middle, grad_attended, kept, sent = middle_step(
        place.reshape(1), attended, mine, goal, keep, vectors, bias_all[None], out_all, up_all, down_all, head_low
    )

    per_block = share // HDIM
    grads = [None] * 4

    def backward(j, after):
        part, output = inputs[j // 2], outputs[j // 2]
        grad = grad_attended[j * share : (j + 1) * share]
        if after is not None:
            grad, after = lax.optimization_barrier((grad, after))
        grads[j] = attention_backward(
            (j % 2) * per_block, per_block, *part, output[0], grad, output[1], output[2]
        )
        return after

    block_rows = share + 2 * deep
    got_core = swap_core(sent)
    kept, sent = fold_core(block_rows, kept, got_core)
    kept = backward(2, kept)
    got_chip = swap_chip(sent)
    backward(3, None)
    kept = fold(kept, got_chip)
    kept = backward(1, kept)
    steps = [1 << k for k in range(size.bit_length() - 1)]
    got = swap_dp(kept, steps[0], size)
    backward(0, None)
    kept = fold(kept, got, last=len(steps) == 1)
    for step in steps[1:]:
        kept = fold(kept, swap_dp(kept, step, size), last=step == steps[-1])
    grad_out = kept[:share]
    grad_up = kept[share : share + deep]
    grad_down = kept[share + deep : block_rows]
    half = HEAD // 2
    head_mine = kept[block_rows : block_rows + half]
    head_other = swap_core(head_mine)
    grad_head = jnp.where(
        core == 0,
        jnp.concatenate([head_mine, head_other], axis=0),
        jnp.concatenate([head_other, head_mine], axis=0),
    )
    small = kept[block_rows + half :]
    loss = small[7, 0]
    grad_up_bias = pick(small[8:12], place)

    all_weights = jnp.concatenate([near, far], axis=1)
    grad_query, grad_key, grad_value = (
        jnp.concatenate([g[k] for g in grads], axis=0) for k in range(3)
    )
    pulled = product(grad_key, all_weights[1], "en,ed->nd") + product(grad_value, all_weights[2], "en,ed->nd")
    query_part = product(grad_query, all_weights[0], "en,ed->nd")
    grad_attn_proj = jnp.stack(
        [
            product(grad_query, first_low[:rows], "en,nd->ed"),
            product(grad_key, first_low, "en,nd->ed"),
            product(grad_value, first_low, "en,nd->ed"),
        ]
    ).reshape(3, 4, share, HEAD)
    other_rows = swap_core(pulled[rows:].astype(bf16)).astype(f32)
    grad_one = pulled[:rows] + query_part + other_rows
    back_one, grad_gain_one, grad_shift_one = norm_backward(grad_one, hat_one, inv_one, vectors[0])
    grad_rows = grad_middle + back_one
    quarter = rows // 2
    returned = swap_chip(grad_rows[quarter:].astype(bf16)).astype(f32)
    grad_frames = jnp.where(
        chip == 0,
        jnp.stack([grad_rows[:quarter], returned]),
        jnp.stack([returned, grad_rows[:quarter]]),
    )
    zeros = jnp.zeros((SMALL - 2, HEAD), f32)
    parts = two_part(jnp.concatenate([grad_gain_one[None], grad_shift_one[None], zeros], axis=0))
    blocks = [grad_attn_proj[:, j].reshape(3 * share, HEAD) for j in range(4)]
    kept = jnp.concatenate([blocks[0], blocks[2], parts], axis=0).astype(bf16)
    sent = jnp.concatenate([blocks[1], blocks[3], parts], axis=0).astype(bf16)
    kept, sent = fold_core(3 * share, kept, swap_core(sent))
    kept = fold(kept, swap_chip(sent))
    for step in steps:
        kept = fold(kept, swap_dp(kept, step, size), last=step == steps[-1])
    grad_attn_proj = jnp.swapaxes(kept[: 3 * share].reshape(3, share, HEAD), 1, 2)
    grad_vectors = jnp.concatenate([kept[3 * share : 3 * share + 2], small[:7]], axis=0)
    first_set = update(attn_proj, momentum_attn, average_attn, grad_attn_proj)
    second_set = update(out_proj, momentum_out, average_out, grad_out)
    third_set = update(up_proj, momentum_up, average_up, grad_up)
    fourth_set = update(up_bias, momentum_bias, average_bias, grad_up_bias)
    fifth_set = update(down_proj, momentum_down, average_down, grad_down)
    sixth_set = update(head_proj, momentum_head, average_head, grad_head)
    seventh_set = update(vectors, momentum_vectors, average_vectors, grad_vectors)
    return (
        loss,
        first_set[0],
        second_set[0],
        third_set[0],
        fourth_set[0],
        fifth_set[0],
        sixth_set[0],
        seventh_set[0],
        first_set[1],
        second_set[1],
        third_set[1],
        fourth_set[1],
        fifth_set[1],
        sixth_set[1],
        seventh_set[1],
        first_set[2],
        second_set[2],
        third_set[2],
        fourth_set[2],
        fifth_set[2],
        sixth_set[2],
        seventh_set[2],
        grad_frames,
    )


def solution(mesh):
    in_specs = (
        P("dp", "tp", None),
        P("dp", "tp", None),
        P("dp", None),
        P("dp", None),
        P(None, None, "tp"),
        P("tp", None),
        P(None, "tp"),
        P("tp"),
        P(None, "tp"),
        P(),
        P(),
        P(None, None, "tp"),
        P("tp", None),
        P(None, "tp"),
        P("tp"),
        P(None, "tp"),
        P(),
        P(),
        P(None, None, "tp"),
        P("tp", None),
        P(None, "tp"),
        P("tp"),
        P(None, "tp"),
        P(),
        P(),
    )
    out_specs = (
        P(),
        P(None, None, "tp"),
        P("tp", None),
        P(None, "tp"),
        P("tp"),
        P(None, "tp"),
        P(),
        P(),
        P(None, None, "tp"),
        P("tp", None),
        P(None, "tp"),
        P("tp"),
        P(None, "tp"),
        P(),
        P(),
        P(None, None, "tp"),
        P("tp", None),
        P(None, "tp"),
        P("tp"),
        P(None, "tp"),
        P(),
        P(),
        P("dp", "tp", None),
    )
    return jax.shard_map(
        per_device, mesh=mesh, in_specs=in_specs, out_specs=out_specs, check_vma=False
    )
```

time: 936 us -> 327 us (0.35)
  waiting for transfers between devices: 395 us -> 71.9 us
  matrix products: 282 us -> 15.6 us
  Pallas kernels: 0 us -> 136 us
  other arithmetic: 126 us -> 33.6 us
  blocking collectives: 62 us -> 0 us
  starting transfers between devices: 1.05 us -> 19.7 us
  between operations: 16 us -> 5.65 us
    dot_general x43 -> x12, matrix products: 282 us -> 15.6 us  [product(): return jnp.einsum(form, left, right, preferred_element_type=jnp.float32)]
    reduce_scatter x4 -> x0, waiting for transfers between devices: 224 us -> none  [the longest x1 63.8 us: per_device(): lax.psum_scatter(product(grad_pre, up_all, 'bsf,df->bsd'), 'tp', scatter_...]
    pallas_call x0 -> x17, Pallas kernels: none -> 136 us  [the longest x4 53 us: attention_backward(): pl.pallas_call(attention_backward_body, grid=(heads,), in_specs=[rows_in,...]
    all_gather x4 -> x0, waiting for transfers between devices: 113 us -> none  [the longest x1 33.5 us: per_device(): first_all = lax.all_gather(first_low, 'tp', axis=1, tiled=True)]
    convert_element_type x9 -> x3, other arithmetic: 78.8 us -> 1.8 us  [the longest x1 1.04 us: per_device(): attn_own = jnp.swapaxes(attn_proj, 1, 2).astype(bf16)]
    ppermute x0 -> x24, waiting for transfers between devices: none -> 71.9 us  [the longest x6 37.2 us: swap_dp(): return lax.ppermute(values, 'dp', [(i, i ^ step) for i in range(size)])]
    psum x2 -> x0, blocking collectives: 62 us -> none  [the longest x1 39.9 us: per_device(): lax.psum((grad_head, grad_vectors, part_loss), ('dp', 'tp'))]
    psum x2 -> x0, waiting for transfers between devices: 58.2 us -> none  [the longest x1 58.2 us: per_device(): lax.psum((grad_attn_proj, grad_out, grad_up, grad_up_bias, grad_down), 'dp')]
  transfers between devices with their start and end apart: 10 -> 24, of which waited for: 9 -> 9; matrix products, arithmetic and copies ran while one was open for 33% -> 22% of each run, Pallas kernels for 0% -> 28%
where the time goes in v1:
time: 327 us; the launch traced here: 323 us
  Pallas kernels  136 us (42%)
  waiting for transfers between devices  71.9 us (22%)
  local copies, waits for them, and re-layouts  40.7 us (12%)
  other arithmetic  33.6 us (10%)
  starting transfers between devices  19.7 us (6%)
  matrix products  15.6 us (5%)
  between operations  5.65 us (2%)
    pallas_call x4, Pallas kernels, attention_backward(): pl.pallas_call(attention_backward_body, grid=(heads,), in_specs=[rows_in,...  53 us
    ppermute x6, waiting for transfers between devices, swap_dp(): return lax.ppermute(values, 'dp', [(i, i ^ step) for i in range(size)])  37.2 us
    pallas_call x2, Pallas kernels, attention_forward(): pl.pallas_call(attention_forward_body, grid=(heads,), in_specs=[pl.BlockS...  35 us
    ppermute x7, waiting for transfers between devices, swap_chip(): return lax.ppermute(values, 'tp', CHIP_PAIRS)  34.6 us
    pallas_call x1, Pallas kernels, middle_step(): pl.pallas_call(middle_body, grid_spec=pltpu.PrefetchScalarGridSpec(num_sc...  24.2 us
    pallas_call x8, Pallas kernels, fold(): pl.pallas_call(fold_body, out_shape=jax.ShapeDtypeStruct(shape.shape, sha...  18.1 us
    unnamed x112, local copies, waits for them, and re-layouts  17 us
    dot_general x12, matrix products, product(): return jnp.einsum(form, left, right, preferred_element_type=jnp.float32)  15.6 us
  transfers between devices with their start and end apart: 24, of which 9 were waited for; matrix products, arithmetic and copies ran while one was open for 22% of the time, Pallas kernels for 28%

profile of v1, /device:TPU:0, one launch (start us, length us, event | category | flops | bytes accessed | tf_op | source)
XLA Modules:
  0.0 323.0 jit_solution(8750753085714423127)
XLA Ops:
  0.7 3.0 collective-permute-start.7
  5.1 2.0 dynamic-slice_bitcast_fusion.3
  7.1 1.8 collective-permute-start.1
  25.0 21.0 %collective-permute-done.5 = bf16[1440,384]{1,0:T(8,128)(2,1)} collective-permute-done((bf16[1440,384]{1,0:T(8,128)(2,1)}, bf16[1440,384]{1,0:T(8,128)(2,1)}, u32[]{:S(2)}, u32[]{:S(2)}) %collective-permute-start.5) | collective-permute-done | bytes 1105952 | tf_op jit(solution)/shard_map/ppermute | solution.py:400
  45.9 2.0 slice.225
  50.5 1.9 fusion.32
  53.9 4.9 %fusion.2 = f32[2304]{0:T(1024)S(1)} fusion(f32[2304]{0:T(1024)S(1)} %broadcast_multiply_fusion, bf16[1152,384]{1,0:T(8,128)(2,1)S(1)} %collective-permute-done.2, bf16[576,384]{1,0:T(8,128)(2,1)S(1)} %collective-permute-done.1, bf16[576,384]{1,0:T(8,128)(2,1)S(1)} %get-tuple-element.127), kind=kLoop, calls=%fused_computation.9 | loop fusion | flops 7960320 | bytes 1787904 | tf_op jit(solution)/shard_map/reduce_sum | solution.py:369
  60.9 1.7 convolution_convert_fusion.1.key
  64.1 2.1 maximum_maximum_fusion
  66.2 17.4 %attention_forward.3 = (bf16[192,1152]{1,0:T(8,128)(2,1)}, f32[4,1,1152]{2,1,0:T(1,128)}, bf16[4,1152,2304]{2,1,0:T(8,128)(2,1)}) custom-call(bf16[192,1152]{1,0:T(8,128)(2,1)} %convolution_convert_fusion.4.query, bf16[192,2304]{1,0:T(8,128)(2,1)} %convolution_convert_fusion.1.key, bf16[256,2304]{1,0:T(8,128)(2,1)} %bitcast.88), custom_call_target="tpu_custom_call" | custom-call | flops 10871635968 | bytes 21233664 | tf_op jit(solution)/shard_map/attention_forward/pallas_call | solution.py:48
  84.8 1.7 convolution_convert_fusion.3.key
  86.5 17.6 %attention_forward.2 = (bf16[192,1152]{1,0:T(8,128)(2,1)}, f32[4,1,1152]{2,1,0:T(1,128)}, bf16[4,1152,2304]{2,1,0:T(8,128)(2,1)}) custom-call(bf16[192,1152]{1,0:T(8,128)(2,1)} %convolution_convert_fusion.5.query, bf16[192,2304]{1,0:T(8,128)(2,1)} %convolution_convert_fusion.3.key, bf16[256,2304]{1,0:T(8,128)(2,1)} %bitcast.85), custom_call_target="tpu_custom_call" | custom-call | flops 10871635968 | bytes 21233664 | tf_op jit(solution)/shard_map/attention_forward/pallas_call | solution.py:48
  104.2 2.3 pad_maximum_fusion.5.attended
  109.2 1.6 pad_maximum_fusion.1
  110.8 24.2 %middle_step.1 = (f32[1152,384]{1,0:T(8,128)}, bf16[384,1152]{1,0:T(8,128)(2,1)}, bf16[1952,384]{1,0:T(8,128)(2,1)}, bf16[1952,384]{1,0:T(8,128)(2,1)}) custom-call(s32[1]{0:T(128)} %bitcast.place, bf16[384,1152]{1,0:T(8,128)(2,1)} %pad_maximum_fusion.5.attended, bf16[1152,384]{1,0:T(8,128)(2,1)} %copy-done.13, bf16[1152,384]{1,0:T(8,128)(2,1)} %pad_maximum_fusion.6.goal, ...), custom_call_target="tpu_custom_call" | custom-call | flops 10192158720 | bytes 5898240 | tf_op jit(solution)/shard_map/middle_step/pallas_call | solution.py:274
  135.1 2.2 fusion.34
  137.8 13.5 %attention_backward.4 = (bf16[96,1152]{1,0:T(8,128)(2,1)}, bf16[96,2304]{1,0:T(8,128)(2,1)}, bf16[96,2304]{1,0:T(8,128)(2,1)}) custom-call(bf16[192,1152]{1,0:T(8,128)(2,1)} %convolution_convert_fusion.5.query, bf16[192,2304]{1,0:T(8,128)(2,1)} %convolution_convert_fusion.3.key, bf16[256,2304]{1,0:T(8,128)(2,1)} %bitcast.86, ...), custom_call_target="tpu_custom_call" | custom-call | flops 10871635968 | bytes 10616832 | tf_op jit(solution)/shard_map/attention_backward/pallas_call | solution.py:101
  151.3 1.8 constant_dynamic-update-slice_fusion.9
  153.1 1.7 constant_dynamic-update-slice_fusion.5
  155.9 13.1 %attention_backward.7 = (bf16[96,1152]{1,0:T(8,128)(2,1)}, bf16[96,2304]{1,0:T(8,128)(2,1)}, bf16[96,2304]{1,0:T(8,128)(2,1)}) custom-call(bf16[192,1152]{1,0:T(8,128)(2,1)} %convolution_convert_fusion.4.query, bf16[192,2304]{1,0:T(8,128)(2,1)} %convolution_convert_fusion.1.key, bf16[256,2304]{1,0:T(8,128)(2,1)} %bitcast.89, ...), custom_call_target="tpu_custom_call" | custom-call | flops 10871635968 | bytes 10616832 | tf_op jit(solution)/shard_map/attention_backward/pallas_call | solution.py:101
  169.0 3.4 %fold_core.2 = (bf16[1088,384]{1,0:T(8,128)(2,1)}, bf16[1088,384]{1,0:T(8,128)(2,1)}) custom-call(bf16[1952,384]{1,0:T(8,128)(2,1)} %get-tuple-element.56.refs_0_, bf16[1952,384]{1,0:T(8,128)(2,1)} %collective-permute-done.11.refs_1_), custom_call_target="tpu_custom_call" | custom-call | flops 749568 | bytes 5996544 | tf_op jit(solution)/shard_map/fold_core/pallas_call | solution.py:330
  172.7 13.1 %attention_backward.6 = (bf16[96,1152]{1,0:T(8,128)(2,1)}, bf16[96,2304]{1,0:T(8,128)(2,1)}, bf16[96,2304]{1,0:T(8,128)(2,1)}) custom-call(bf16[192,1152]{1,0:T(8,128)(2,1)} %convolution_convert_fusion.4.query, bf16[192,2304]{1,0:T(8,128)(2,1)} %convolution_convert_fusion.1.key, bf16[256,2304]{1,0:T(8,128)(2,1)} %bitcast.90, ...), custom_call_target="tpu_custom_call" | custom-call | flops 10871635968 | bytes 10616832 | tf_op jit(solution)/shard_map/attention_backward/pallas_call | solution.py:101
  185.8 7.5 %collective-permute-done.12.right = bf16[1088,384]{1,0:T(8,128)(2,1)} collective-permute-done((bf16[1088,384]{1,0:T(8,128)(2,1)}, bf16[1088,384]{1,0:T(8,128)(2,1)}, u32[]{:S(2)}, u32[]{:S(2)}) %collective-permute-start.12) | collective-permute-done | bytes 835616 | tf_op jit(solution)/shard_map/ppermute | solution.py:400
  193.2 2.6 fold.8.left
  195.8 13.3 %attention_backward.5 = (bf16[96,1152]{1,0:T(8,128)(2,1)}, bf16[96,2304]{1,0:T(8,128)(2,1)}, bf16[96,2304]{1,0:T(8,128)(2,1)}) custom-call(bf16[192,1152]{1,0:T(8,128)(2,1)} %convolution_convert_fusion.5.query, bf16[192,2304]{1,0:T(8,128)(2,1)} %convolution_convert_fusion.3.key, bf16[256,2304]{1,0:T(8,128)(2,1)} %bitcast.87, ...), custom_call_target="tpu_custom_call" | custom-call | flops 10871635968 | bytes 10616832 | tf_op jit(solution)/shard_map/attention_backward/pallas_call | solution.py:101
  209.1 1.6 collective-permute-start.13
  210.7 1.8 constant_dynamic-update-slice_fusion.8
  212.5 1.8 constant_dynamic-update-slice_fusion.7
  215.2 2.6 fusion.37
  227.3 1.9 collective-permute-done.13.right
  229.1 2.5 fold.9.left
  231.7 1.6 collective-permute-start.14
  234.0 2.1 fold_core.3
  236.6 5.9 %collective-permute-done.18.right = bf16[320,384]{1,0:T(8,128)(2,1)S(1)} collective-permute-done((bf16[320,384]{1,0:T(8,128)(2,1)}, bf16[320,384]{1,0:T(8,128)(2,1)S(1)}, u32[]{:S(2)}, u32[]{:S(2)}) %collective-permute-start.18) | collective-permute-done | bytes 245792 | tf_op jit(solution)/shard_map/ppermute | solution.py:400
  243.2 1.8 fold.12.left
  246.5 2.3 multiply_add_fusion
  251.9 2.5 fold.10.left
  254.4 2.6 collective-permute-start.15
  257.7 1.8 fold.13.left
  259.5 1.6 collective-permute-start.20
  261.2 17.2 %collective-permute-done.20.right = bf16[320,384]{1,0:T(8,128)(2,1)S(1)} collective-permute-done((bf16[320,384]{1,0:T(8,128)(2,1)}, bf16[320,384]{1,0:T(8,128)(2,1)S(1)}, u32[]{:S(2)}, u32[]{:S(2)}) %collective-permute-start.20) | collective-permute-done | bytes 245792 | tf_op jit(solution)/shard_map/ppermute | solution.py:404
  279.0 1.8 fold.14.left
  280.8 2.3 collective-permute-start.21
  285.5 16.6 %collective-permute-done.21.right = bf16[320,384]{1,0:T(8,128)(2,1)S(1)} collective-permute-done((bf16[320,384]{1,0:T(8,128)(2,1)}, bf16[320,384]{1,0:T(8,128)(2,1)S(1)}, u32[]{:S(2)}, u32[]{:S(2)}) %collective-permute-start.21) | collective-permute-done | bytes 245792 | tf_op jit(solution)/shard_map/ppermute | solution.py:404
  302.9 1.9 fold.15
  308.0 3.1 fold.11
  314.5 3.4 %multiply_add_fusion.2 = (f32[384,384]{1,0:T(8,128)}, f32[384,384]{1,0:T(8,128)}, f32[384,384]{1,0:T(8,128)}, f32[384,384]{1,0:T(8,128)}, f32[384,384]{1,0:T(8,128)}, /*index=5*/f32[384,384]{1,0:T(8,128)}) fusion(f32[384,384]{1,0:T(8,128)S(1)} %copy-done.17, f32[384,384]{1,0:T(8,128)S(1)} %copy-done.2, f32[1072,384]{1,0:T(8,128)} %fold.11, ...), kind=kLoop, calls=%fused_computation.45 | loop fusion | flops 2654208 | bytes 8257536 | tf_op jit(solution)/shard_map/add | solution.py:387
  319.7 1.7 multiply_add_fusion.9
  (219 shorter events, 57.6 us)
Async XLA Ops:
  0.7 8.2 %copy-start.49 = (s32[1,2]{1,0:T(1,128)S(1)}, s32[1,2]{1,0:T(1,128)}, u32[]{:S(2)}) copy-start(s32[1,2]{1,0:T(1,128)} %param.28) | copy-start | bytes 28
  0.7 11.4 %copy-start.23 = (f32[96,384]{1,0:T(8,128)S(1)}, f32[96,384]{1,0:T(8,128)}, u32[]{:S(2)}) copy-start(f32[96,384]{1,0:T(8,128)} %param.30) | copy-start | bytes 442372
  0.7 11.4 %copy-start.3 = (f32[384,384]{1,0:T(8,128)S(1)}, f32[384,384]{1,0:T(8,128)}, u32[]{:S(2)}) copy-start(f32[384,384]{1,0:T(8,128)} %param.31) | copy-start | bytes 1769476
  0.7 11.4 %copy-start.1 = (f32[384,384]{1,0:T(8,128)S(1)}, f32[384,384]{1,0:T(8,128)}, u32[]{:S(2)}) copy-start(f32[384,384]{1,0:T(8,128)} %param.33) | copy-start | bytes 1769476
  0.7 17.1 %collective-permute-start.7 = (f32[384]{0:T(512)}, f32[384]{0:T(512)S(1)}, u32[]{:S(2)}, u32[]{:S(2)}) collective-permute-start(f32[384]{0:T(512)} %param.32), channel_id=1, source_target_pairs={{0,2},{2,0},{1,3},{3,1},{4,6},{6,4},{5,7},{7,5},{8,10},{10,8},{9,1... | collective-permute-start | bytes 4616 | tf_op jit(solution)/shard_map/ppermute | solution.py:400
  3.7 15.9 %collective-permute-start.6 = (f32[384]{0:T(512)}, f32[384]{0:T(512)S(1)}, u32[]{:S(2)}, u32[]{:S(2)}) collective-permute-start(f32[384]{0:T(512)} %param.32), channel_id=1, source_target_pairs={{0,1},{1,0},{2,3},{3,2},{4,5},{5,4},{6,7},{7,6},{8,9},{9,8},{10,11... | collective-permute-start | bytes 4616 | tf_op jit(solution)/shard_map/ppermute | solution.py:396
  4.8 16.1 %collective-permute-start.3 = (bf16[3,96,384]{2,1,0:T(8,128)(2,1)S(1)}, bf16[3,96,384]{2,1,0:T(8,128)(2,1)}, u32[]{:S(2)}, u32[]{:S(2)}) collective-permute-start(bf16[3,96,384]{2,1,0:T(8,128)(2,1)S(1)} %convert_bitcast_fusion), channel_id=1, source_target_pairs={{0,2},{2,0},{1,3},{3,1},{4,6},{6,4},{5,7},{7,5},{8,10},{10,8},{9,1... | collective-permute-start | bytes 663560 | tf_op jit(solution)/shard_map/ppermute | solution.py:400
  7.1 15.5 %collective-permute-start.1 = (bf16[576,384]{1,0:T(8,128)(2,1)}, bf16[576,384]{1,0:T(8,128)(2,1)S(1)}, u32[]{:S(2)}, u32[]{:S(2)}) collective-permute-start(bf16[576,384]{1,0:T(8,128)(2,1)} %get-tuple-element.128), channel_id=1, source_target_pairs={{0,2},{2,0},{1,3},{3,1},{4,6},{6,4},{5,7},{7,5},{8,10},{10,8},{9,1... | collective-permute-start | bytes 1327112 | tf_op jit(solution)/shard_map/ppermute | solution.py:400
  15.8 30.1 %collective-permute-start.5 = (bf16[1440,384]{1,0:T(8,128)(2,1)}, bf16[1440,384]{1,0:T(8,128)(2,1)}, u32[]{:S(2)}, u32[]{:S(2)}) collective-permute-start(bf16[1440,384]{1,0:T(8,128)(2,1)} %pad_maximum_fusion.3), channel_id=1, source_target_pairs={{0,2},{2,0},{1,3},{3,1},{4,6},{6,4},{5,7},{7,5},{8,10},{10,8},{9,1... | collective-permute-start | bytes 3317768 | tf_op jit(solution)/shard_map/ppermute | solution.py:400
  17.8 2.3 collective-permute-start.8
  19.6 3.2 collective-permute-start
  20.1 3.8 %collective-permute-start.9 = (bf16[864,384]{1,0:T(8,128)(2,1)}, bf16[864,384]{1,0:T(8,128)(2,1)S(1)}, u32[]{:S(2)}, u32[]{:S(2)}) collective-permute-start(bf16[864,384]{1,0:T(8,128)(2,1)} %pad_maximum_fusion.8), channel_id=1, source_target_pairs={{0,1},{1,0},{2,3},{3,2},{4,5},{5,4},{6,7},{7,6},{8,9},{9,8},{10,11... | collective-permute-start | bytes 1990664 | tf_op jit(solution)/shard_map/ppermute | solution.py:396
  20.8 1.9 collective-permute-start.4
  22.6 25.3 %copy-start.13 = (bf16[1152,384]{1,0:T(8,128)(2,1)}, bf16[1152,384]{1,0:T(8,128)(2,1)S(1)}, u32[]{:S(2)}) copy-start(bf16[1152,384]{1,0:T(8,128)(2,1)S(1)} %pad_maximum_fusion.4.frames) | copy-start | bytes 2654212
  22.6 30.9 %collective-permute-start.2 = (bf16[1152,384]{1,0:T(8,128)(2,1)S(1)}, bf16[1152,384]{1,0:T(8,128)(2,1)S(1)}, u32[]{:S(2)}, u32[]{:S(2)}) collective-permute-start(bf16[1152,384]{1,0:T(8,128)(2,1)S(1)} %pad_maximum_fusion.4.frames), channel_id=1, source_target_pairs={{0,1},{1,0},{2,3},{3,2},{4,5},{5,4},{6,7},{7,6},{8,9},{9,8},{10,11... | collective-permute-start | bytes 2654216 | tf_op jit(solution)/shard_map/ppermute | solution.py:396
  24.0 26.6 %copy-start.16 = (bf16[864,384]{1,0:T(8,128)(2,1)}, bf16[864,384]{1,0:T(8,128)(2,1)S(1)}, u32[]{:S(2)}) copy-start(bf16[864,384]{1,0:T(8,128)(2,1)S(1)} %collective-permute-done.9) | copy-start | bytes 1990660
  47.9 58.5 %collective-permute-start.10 = (bf16[864,384]{1,0:T(8,128)(2,1)}, bf16[864,384]{1,0:T(8,128)(2,1)}, u32[]{:S(2)}, u32[]{:S(2)}) collective-permute-start(bf16[864,384]{1,0:T(8,128)(2,1)} %slice.225), channel_id=1, source_target_pairs={{0,1},{1,0},{2,3},{3,2},{4,5},{5,4},{6,7},{7,6},{8,9},{9,8},{10,11... | collective-permute-start | bytes 1990664 | tf_op jit(solution)/shard_map/ppermute | solution.py:396
  58.9 168.4 %copy-start.42 = (f32[2304]{0:T(1024)}, f32[2304]{0:T(1024)S(1)}, u32[]{:S(2)}) copy-start(f32[2304]{0:T(1024)S(1)} %add_rsqrt_fusion) | copy-start | bytes 27652
  137.3 31.7 %collective-permute-start.11 = (bf16[1952,384]{1,0:T(8,128)(2,1)}, bf16[1952,384]{1,0:T(8,128)(2,1)}, u32[]{:S(2)}, u32[]{:S(2)}) collective-permute-start(bf16[1952,384]{1,0:T(8,128)(2,1)} %get-tuple-element.57), channel_id=1, source_target_pairs={{0,1},{1,0},{2,3},{3,2},{4,5},{5,4},{6,7},{7,6},{8,9},{9,8},{10,11... | collective-permute-start | bytes 4497416 | tf_op jit(solution)/shard_map/ppermute | solution.py:396
  172.4 20.8 %collective-permute-start.12 = (bf16[1088,384]{1,0:T(8,128)(2,1)}, bf16[1088,384]{1,0:T(8,128)(2,1)}, u32[]{:S(2)}, u32[]{:S(2)}) collective-permute-start(bf16[1088,384]{1,0:T(8,128)(2,1)} %get-tuple-element.60), channel_id=1, source_target_pairs={{0,2},{2,0},{1,3},{3,1},{4,6},{6,4},{5,7},{7,5},{8,10},{10,8},{9,1... | collective-permute-start | bytes 2506760 | tf_op jit(solution)/shard_map/ppermute | solution.py:400
  209.1 20.0 %collective-permute-start.13 = (bf16[1088,384]{1,0:T(8,128)(2,1)}, bf16[1088,384]{1,0:T(8,128)(2,1)}, u32[]{:S(2)}, u32[]{:S(2)}) collective-permute-start(bf16[1088,384]{1,0:T(8,128)(2,1)} %fold.8.left), channel_id=1, source_target_pairs={{0,4},{4,0},{8,12},{12,8},{16,20},{20,16},{24,28},{28,24},{1,5},{5... | collective-permute-start | bytes 2506760 | tf_op jit(solution)/shard_map/ppermute | solution.py:404
  221.8 3.2 collective-permute-start.16
  227.2 6.0 %collective-permute-start.17 = (bf16[608,384]{1,0:T(8,128)(2,1)S(1)}, bf16[608,384]{1,0:T(8,128)(2,1)S(1)}, u32[]{:S(2)}, u32[]{:S(2)}) collective-permute-start(bf16[608,384]{1,0:T(8,128)(2,1)S(1)} %get-tuple-element.133), channel_id=1, source_target_pairs={{0,1},{1,0},{2,3},{3,2},{4,5},{5,4},{6,7},{7,6},{8,9},{9,8},{10,11... | collective-permute-start | bytes 1400840 | tf_op jit(solution)/shard_map/ppermute | solution.py:396
  227.3 19.3 %slice-start.2 = ((f32[2304]{0:T(1024)}), f32[1152]{0:T(1024)S(1)}, s32[]{:S(2)}) async-start(f32[2304]{0:T(1024)} %copy-done.42), calls=%async_computation.2 | async-start | bytes 16384 | tf_op jit(solution)/shard_map/slice | solution.py:486
  231.7 19.3 %collective-permute-start.14 = (bf16[1088,384]{1,0:T(8,128)(2,1)}, bf16[1088,384]{1,0:T(8,128)(2,1)S(1)}, u32[]{:S(2)}, u32[]{:S(2)}) collective-permute-start(bf16[1088,384]{1,0:T(8,128)(2,1)} %fold.9.left), channel_id=1, source_target_pairs={{0,8},{4,12},{8,0},{12,4},{16,24},{20,28},{24,16},{28,20},{1,9},{5... | collective-permute-start | bytes 2506760 | tf_op jit(solution)/shard_map/ppermute | solution.py:404
  236.1 6.4 %collective-permute-start.18 = (bf16[320,384]{1,0:T(8,128)(2,1)}, bf16[320,384]{1,0:T(8,128)(2,1)S(1)}, u32[]{:S(2)}, u32[]{:S(2)}) collective-permute-start(bf16[320,384]{1,0:T(8,128)(2,1)} %get-tuple-element.81), channel_id=1, source_target_pairs={{0,2},{2,0},{1,3},{3,1},{4,6},{6,4},{5,7},{7,5},{8,10},{10,8},{9,1... | collective-permute-start | bytes 737288 | tf_op jit(solution)/shard_map/ppermute | solution.py:400
  245.0 12.0 %collective-permute-start.19 = (bf16[320,384]{1,0:T(8,128)(2,1)}, bf16[320,384]{1,0:T(8,128)(2,1)S(1)}, u32[]{:S(2)}, u32[]{:S(2)}) collective-permute-start(bf16[320,384]{1,0:T(8,128)(2,1)} %fold.12.left), channel_id=1, source_target_pairs={{0,4},{4,0},{8,12},{12,8},{16,20},{20,16},{24,28},{28,24},{1,5},{5... | collective-permute-start | bytes 737288 | tf_op jit(solution)/shard_map/ppermute | solution.py:404
  248.9 34.2 %collective-permute-start.23 = (bf16[576,384]{1,0:T(8,128)(2,1)S(1)}, bf16[576,384]{1,0:T(8,128)(2,1)}, u32[]{:S(2)}, u32[]{:S(2)}) collective-permute-start(bf16[576,384]{1,0:T(8,128)(2,1)S(1)} %slice.309), channel_id=1, source_target_pairs={{0,2},{2,0},{1,3},{3,1},{4,6},{6,4},{5,7},{7,5},{8,10},{10,8},{9,1... | collective-permute-start | bytes 1327112 | tf_op jit(solution)/shard_map/ppermute | solution.py:400
  254.4 52.7 %collective-permute-start.15 = (bf16[1088,384]{1,0:T(8,128)(2,1)}, bf16[1088,384]{1,0:T(8,128)(2,1)S(1)}, u32[]{:S(2)}, u32[]{:S(2)}) collective-permute-start(bf16[1088,384]{1,0:T(8,128)(2,1)} %fold.10.left), channel_id=1, source_target_pairs={{0,16},{4,20},{8,24},{12,28},{16,0},{20,4},{24,8},{28,12},{1,17},{... | collective-permute-start | bytes 2506760 | tf_op jit(solution)/shard_map/ppermute | solution.py:404
  259.5 18.8 %collective-permute-start.20 = (bf16[320,384]{1,0:T(8,128)(2,1)}, bf16[320,384]{1,0:T(8,128)(2,1)S(1)}, u32[]{:S(2)}, u32[]{:S(2)}) collective-permute-start(bf16[320,384]{1,0:T(8,128)(2,1)} %fold.13.left), channel_id=1, source_target_pairs={{0,8},{4,12},{8,0},{12,4},{16,24},{20,28},{24,16},{28,20},{1,9},{5... | collective-permute-start | bytes 737288 | tf_op jit(solution)/shard_map/ppermute | solution.py:404
  280.8 21.3 %collective-permute-start.21 = (bf16[320,384]{1,0:T(8,128)(2,1)}, bf16[320,384]{1,0:T(8,128)(2,1)S(1)}, u32[]{:S(2)}, u32[]{:S(2)}) collective-permute-start(bf16[320,384]{1,0:T(8,128)(2,1)} %fold.14.left), channel_id=1, source_target_pairs={{0,16},{4,20},{8,24},{12,28},{16,0},{20,4},{24,8},{28,12},{1,17},{... | collective-permute-start | bytes 737288 | tf_op jit(solution)/shard_map/ppermute | solution.py:404
  285.5 20.3 %copy-start.7 = (f32[3,384,96]{1,2,0:T(8,128)S(1)}, f32[3,384,96]{1,2,0:T(8,128)}, u32[]{:S(2)}) copy-start(f32[3,384,96]{1,2,0:T(8,128)} %param.29) | copy-start | bytes 1327108
  285.5 20.3 %copy-start.26 = (f32[3,384,96]{1,2,0:T(8,128)S(1)}, f32[3,384,96]{1,2,0:T(8,128)}, u32[]{:S(2)}) copy-start(f32[3,384,96]{1,2,0:T(8,128)} %param.43) | copy-start | bytes 1327108
  285.5 20.3 %copy-start.27 = (f32[3,384,96]{1,2,0:T(8,128)S(1)}, f32[3,384,96]{1,2,0:T(8,128)}, u32[]{:S(2)}) copy-start(f32[3,384,96]{1,2,0:T(8,128)} %param.36) | copy-start | bytes 1327108
  307.0 6.7 %slice-start = ((f32[304,384]{1,0:T(8,128)}), f32[2,384]{1,0:T(2,128)S(1)}, s32[]{:S(2)}) async-start(f32[304,384]{1,0:T(8,128)} %fold.15), calls=%async_computation | async-start | bytes 6144 | tf_op jit(solution)/shard_map/slice | solution.py:582
  307.0 6.7 %copy-start.43 = (f32[9,384]{1,0:T(8,128)S(1)}, f32[9,384]{1,0:T(8,128)}, u32[]{:S(2)}) copy-start(f32[9,384]{1,0:T(8,128)} %vectors.1) | copy-start | bytes 41476
  307.0 6.7 %copy-start.44 = (f32[9,384]{1,0:T(8,128)S(1)}, f32[9,384]{1,0:T(8,128)}, u32[]{:S(2)}) copy-start(f32[9,384]{1,0:T(8,128)} %param.49) | copy-start | bytes 41476
  307.0 6.7 %copy-start.45 = (f32[9,384]{1,0:T(8,128)S(1)}, f32[9,384]{1,0:T(8,128)}, u32[]{:S(2)}) copy-start(f32[9,384]{1,0:T(8,128)} %param.42) | copy-start | bytes 41476
  307.0 7.3 %copy-start.2 = (f32[384,384]{1,0:T(8,128)S(1)}, f32[384,384]{1,0:T(8,128)}, u32[]{:S(2)}) copy-start(f32[384,384]{1,0:T(8,128)} %param.33) | copy-start | bytes 1769476
  307.0 7.3 %copy-start.4 = (f32[384,384]{1,0:T(8,128)S(1)}, f32[384,384]{1,0:T(8,128)}, u32[]{:S(2)}) copy-start(f32[384,384]{1,0:T(8,128)} %param.31) | copy-start | bytes 1769476
  307.1 7.3 %copy-start.17 = (f32[384,384]{1,0:T(8,128)S(1)}, f32[384,384]{1,0:T(8,128)}, u32[]{:S(2)}) copy-start(f32[384,384]{1,0:T(8,128)} %param.47) | copy-start | bytes 1769476
  307.1 7.3 %copy-start.18 = (f32[384,384]{1,0:T(8,128)S(1)}, f32[384,384]{1,0:T(8,128)}, u32[]{:S(2)}) copy-start(f32[384,384]{1,0:T(8,128)} %param.40) | copy-start | bytes 1769476
  307.1 7.3 %copy-start.19 = (f32[384,384]{1,0:T(8,128)S(1)}, f32[384,384]{1,0:T(8,128)}, u32[]{:S(2)}) copy-start(f32[384,384]{1,0:T(8,128)} %param.38) | copy-start | bytes 1769476
  307.1 7.3 %copy-start.20 = (f32[384,384]{1,0:T(8,128)S(1)}, f32[384,384]{1,0:T(8,128)}, u32[]{:S(2)}) copy-start(f32[384,384]{1,0:T(8,128)} %param.45) | copy-start | bytes 1769476
  313.6 7.8 %collective-permute-start.22 = (f32[192,384]{1,0:T(8,128)S(1)}, f32[192,384]{1,0:T(8,128)S(1)}, u32[]{:S(2)}, u32[]{:S(2)}) collective-permute-start(f32[192,384]{1,0:T(8,128)S(1)} %slice.249), channel_id=1, source_target_pairs={{0,1},{1,0},{2,3},{3,2},{4,5},{5,4},{6,7},{7,6},{8,9},{9,8},{10,11... | collective-permute-start | bytes 884744 | tf_op jit(solution)/shard_map/ppermute | solution.py:396
  314.5 6.9 %copy-start.6 = (f32[384,384]{1,0:T(8,128)S(1)}, f32[384,384]{1,0:T(8,128)}, u32[]{:S(2)}) copy-start(f32[384,384]{1,0:T(8,128)} %param.34) | copy-start | bytes 1769476
  314.5 6.9 %copy-start.21 = (f32[384,384]{1,0:T(8,128)S(1)}, f32[384,384]{1,0:T(8,128)}, u32[]{:S(2)}) copy-start(f32[384,384]{1,0:T(8,128)} %param.48) | copy-start | bytes 1769476
  314.5 6.9 %copy-start.22 = (f32[384,384]{1,0:T(8,128)S(1)}, f32[384,384]{1,0:T(8,128)}, u32[]{:S(2)}) copy-start(f32[384,384]{1,0:T(8,128)} %param.41) | copy-start | bytes 1769476
  (30 other events, 85.6 us)
